TPU v7x, 32 devices: a whole 2x2x4 slice. The times are simulated.
32 devices in a mesh: dp: 8 (over z, x), expert: 4 (over y, core).
Axes of the slice: x: 2, y: 2, z: 4, core: 2. Of those that a mesh axis runs over, the one named last changes fastest.
Arguments:
- tokens: bfloat16 [4096, 1024], P(('dp', 'expert')), may hold values from -6 to 6
- expert_ids: int32 [4096, 8], P(('dp', 'expert')), may hold values from 0 to 15, as said below
- slot_index: int32 [4096, 8], P(('dp', 'expert')), may hold values from -1 to 63, as said below
- combine_weight: bfloat16 [4096, 8], P(('dp', 'expert')), may hold values from 0.099609375 to 0.8984375
- talker_owner: int32 [4096], P(('dp', 'expert')), may hold values from 0 to 7, as said below
- gate_weight: bfloat16 [16, 1024, 384], P('expert'), may hold values from -0.1875 to 0.1875
- up_weight: bfloat16 [16, 1024, 384], P('expert'), may hold values from -0.1875 to 0.1875
- down_weight: bfloat16 [16, 1024, 384], P('expert'), may hold values from -0.3125 to 0.3125
- grad_talker: bfloat16 [4096, 1024], P(('dp', 'expert')), may hold values from -3 to 3
Outputs:
- talker_out: bfloat16 [4096, 1024], P(('dp', 'expert'))
- grad_tokens: bfloat16 [4096, 1024], P(('dp', 'expert'))
- grad_gate: float32 [16, 1024, 384], P('expert', 'dp')
- grad_up: float32 [16, 1024, 384], P('expert', 'dp')
- grad_down: float32 [16, 1024, 384], P('expert', 'dp')
Inputs may be any that keep to these rules, and one draw needn't show every extreme that they name: `expert_ids`: each row names 8 different experts; one expert is named by every row. `slot_index`: for the pairs of one device's 128 rows that name one expert, taken in row order, the slot is the pair's rank among them when under 64, else -1; on every device some expert fills all 64 slots. `talker_owner`: among one device's 128 rows each owner appears exactly 16 times.
All inputs are finite; a program needn't handle non-finite values.
Results may differ from a plain program's by a relative error of at most 0.02.
Values may be sent and summed in bfloat16 or wider, within the bound.
A program may use at most 64 MiB of HBM per device.

v0:
```python
import jax
import jax.numpy as jnp
from jax import lax
from jax.sharding import PartitionSpec as P

EXPERTS = 16
CAP = 64


def padded(values):
    return jnp.concatenate([values, jnp.zeros((1,) + values.shape[1:], values.dtype)], 0)


def slot_table(route_ids, route_slots, first_expert, selected, blocks):
    row_count, pair_width = route_ids.shape
    per_block = row_count // blocks
    block_of = (jnp.arange(row_count, dtype=jnp.int32) // per_block)[:, None]
    local_index = route_ids - first_expert
    usable = (route_slots >= 0) & (local_index >= 0) & (local_index < selected)
    slot_count = blocks * selected * CAP
    position = jnp.where(
        usable, block_of * (selected * CAP) + local_index * CAP + route_slots, slot_count
    )
    pair_table = jnp.full((slot_count + 1,), row_count * pair_width, jnp.int32)
    pair_table = pair_table.at[position.reshape(-1)].set(
        jnp.arange(row_count * pair_width, dtype=jnp.int32)
    )
    return (pair_table[:slot_count], position)


def owner_position(owner_ids, owner_count, per_owner):
    onehot = (owner_ids[:, None] == jnp.arange(owner_count, dtype=jnp.int32)[None, :]).astype(
        jnp.int32
    )
    before = jnp.cumsum(onehot, axis=0, dtype=jnp.int32) - onehot
    ranked = jnp.sum(before * onehot, axis=1, dtype=jnp.int32)
    return owner_ids * per_owner + ranked


def expert_forward(inputs, gate_weight, up_weight, down_weight):
    gate_pre = jnp.einsum("sekd,edf->sekf", inputs, gate_weight, preferred_element_type=jnp.float32)
    up_pre = jnp.einsum("sekd,edf->sekf", inputs, up_weight, preferred_element_type=jnp.float32)
    hidden = (jax.nn.silu(gate_pre) * up_pre).astype(jnp.bfloat16)
    outputs = jnp.einsum(
        "sekf,edf->sekd", hidden, down_weight, preferred_element_type=jnp.float32
    ).astype(jnp.bfloat16)
    return (gate_pre, up_pre, hidden, outputs)


def on_device(
    tokens,
    expert_ids,
    slot_index,
    combine_weight,
    talker_owner,
    gate_weight,
    up_weight,
    down_weight,
    grad_talker,
):
    expert_devs = lax.axis_size("expert")
    data_devs = lax.axis_size("dp")
    local_experts = gate_weight.shape[0]
    tok_rows, model_width = tokens.shape
    pair_width = expert_ids.shape[1]
    slot_shape = (expert_devs, local_experts, CAP, model_width)
    source_table, source_position = slot_table(expert_ids, slot_index, 0, EXPERTS, 1)
    send_rows = padded(tokens)[source_table // pair_width].reshape(slot_shape)
    arrived = lax.all_to_all(send_rows, "expert", split_axis=0, concat_axis=0, tiled=True)
    gate_pre, up_pre, forward_hidden, outputs = expert_forward(
        arrived, gate_weight, up_weight, down_weight
    )
    home_rows = lax.all_to_all(outputs, "expert", split_axis=0, concat_axis=0, tiled=True)
    returned, inputs, gate_pre, up_pre, hidden = (
        home_rows,
        arrived,
        gate_pre,
        up_pre,
        forward_hidden,
    )
    flat_home = padded(returned.reshape(-1, model_width))
    picked = flat_home[source_position]
    mixed_rows = jnp.einsum(
        "tk,tkd->td", combine_weight, picked, preferred_element_type=jnp.float32
    ).astype(jnp.bfloat16)
    per_owner = tok_rows // data_devs
    owner_slot = owner_position(talker_owner, data_devs, per_owner)
    inverse = (
        jnp.zeros((tok_rows,), jnp.int32).at[owner_slot].set(jnp.arange(tok_rows, dtype=jnp.int32))
    )
    owner_rows = mixed_rows[inverse].reshape(data_devs, per_owner, model_width)
    talker_out = lax.all_to_all(owner_rows, "dp", split_axis=0, concat_axis=0, tiled=True).reshape(
        tok_rows, model_width
    )
    owner_grads = grad_talker.reshape(data_devs, per_owner, model_width)
    arrived_grads = lax.all_to_all(
        owner_grads, "dp", split_axis=0, concat_axis=0, tiled=True
    ).reshape(tok_rows, model_width)
    upstream = arrived_grads[owner_slot]
    weight_slots = padded(combine_weight.reshape(-1))[source_table]
    grad_rows = padded(upstream)[source_table // pair_width]
    sending = (grad_rows.astype(jnp.float32) * weight_slots.astype(jnp.float32)[:, None]).astype(
        jnp.bfloat16
    )
    grad_out = lax.all_to_all(
        sending.reshape(slot_shape), "expert", split_axis=0, concat_axis=0, tiled=True
    )
    grad_hidden = jnp.einsum(
        "sekd,edf->sekf", grad_out, down_weight, preferred_element_type=jnp.float32
    )
    sigmoid_gate = jax.nn.sigmoid(gate_pre)
    grad_up_pre = (grad_hidden * gate_pre * sigmoid_gate).astype(jnp.bfloat16)
    grad_gate_pre = (
        grad_hidden * up_pre * sigmoid_gate * (1.0 + gate_pre * (1.0 - sigmoid_gate))
    ).astype(jnp.bfloat16)
    grad_in = jnp.einsum(
        "sekf,edf->sekd", grad_gate_pre, gate_weight, preferred_element_type=jnp.float32
    )
    grad_in = grad_in + jnp.einsum(
        "sekf,edf->sekd", grad_up_pre, up_weight, preferred_element_type=jnp.float32
    )
    grad_home = lax.all_to_all(
        grad_in.astype(jnp.bfloat16), "expert", split_axis=0, concat_axis=0, tiled=True
    )
    flat_grads = padded(grad_home.reshape(-1, model_width))
    unit_weights = jnp.ones(expert_ids.shape, jnp.bfloat16)
    grad_tokens = jnp.einsum(
        "tk,tkd->td", unit_weights, flat_grads[source_position], preferred_element_type=jnp.float32
    ).astype(jnp.bfloat16)
    factor = 1.0 / data_devs
    column_piece = inputs
    gate_term = jnp.einsum(
        "sekd,sekf->def", column_piece, grad_gate_pre, preferred_element_type=jnp.float32
    )
    up_term = jnp.einsum(
        "sekd,sekf->def", column_piece, grad_up_pre, preferred_element_type=jnp.float32
    )
    pair_terms = jnp.stack((gate_term, up_term), 1)
    column_piece = grad_out
    weight_totals = lax.psum_scatter(
        jnp.concatenate(
            [
                pair_terms,
                jnp.einsum(
                    "sekd,sekf->def", column_piece, hidden, preferred_element_type=jnp.float32
                )[:, None],
            ],
            1,
        ).astype(jnp.bfloat16),
        "dp",
        scatter_dimension=0,
        tiled=True,
    ).astype(jnp.float32)
    grad_gate = weight_totals[:, 0].transpose(1, 0, 2) * factor
    grad_up = weight_totals[:, 1].transpose(1, 0, 2) * factor
    grad_down = weight_totals[:, 2].transpose(1, 0, 2) * factor
    return (talker_out, grad_tokens, grad_gate, grad_up, grad_down)


def solution(mesh):
    placed = (
        P(("dp", "expert"), None),
        P(("dp", "expert"), None),
        P(("dp", "expert"), None),
        P(("dp", "expert"), None),
        P(("dp", "expert")),
        P("expert", None, None),
        P("expert", None, None),
        P("expert", None, None),
        P(("dp", "expert"), None),
    )
    return jax.shard_map(
        on_device,
        mesh=mesh,
        in_specs=placed,
        out_specs=(
            P(("dp", "expert"), None),
            P(("dp", "expert"), None),
            P("expert", "dp", None),
            P("expert", "dp", None),
            P("expert", "dp", None),
        ),
        check_vma=False,
    )
```

profile of v0, /device:TPU:0, one launch (start us, length us, event | category | flops | bytes accessed | tf_op | source)
XLA Modules:
  0.0 307.0 jit_solution(13472130957315981880)
XLA Ops:
  7.2 7.5 %all-to-all-start.3 = ((bf16[8,16,1024]{2,1,0:T(8,128)(2,1)}), bf16[8,16,1024]{2,1,0:T(8,128)(2,1)}, u32[]{:S(2)}, u32[]{:S(2)}) async-start(bf16[8,16,1024]{2,1,0:T(8,128)(2,1)} %bitcast.151), calls=%async_computation.3 | async-start | bytes 524288 | tf_op jit(solution)/shard_map/all_to_all | solution.py:96
  15.6 1.0 concatenate.19
  16.6 4.3 %scatter_custom_fusion = s32[1025]{0:T(1024)S(1)} fusion(s32[1024]{0:T(1024)S(1)} %bitcast.153, s32[1024]{0:T(1024)S(1)} %iota.16, s32[]{:T(128)} %constant.29.clone.1), kind=kCustom, calls=%fused_computation.87 | custom fusion | bytes 4104 | tf_op jit(solution)/shard_map/scatter | solution.py:25
  21.0 5.4 %gather_fusion = bf16[1024,1024]{1,0:T(8,128)(2,1)} fusion(bf16[129,1024]{1,0:T(8,128)(2,1)S(1)} %concatenate.19, s32[1024]{0:T(1024)S(1)} %get-tuple-element.34), kind=kCustom, calls=%fused_computation | custom fusion | bytes 4198400 | tf_op jit(solution)/shard_map/gather | solution.py:68
  26.4 4.6 %all-to-all-start = ((bf16[4,4,64,1024]{3,2,1,0:T(8,128)(2,1)}), bf16[4,4,64,1024]{3,2,1,0:T(8,128)(2,1)}, u32[]{:S(2)}, u32[]{:S(2)}) async-start(bf16[4,4,64,1024]{3,2,1,0:T(8,128)(2,1)} %bitcast.146), calls=%async_computation | async-start | bytes 4194304 | tf_op jit(solution)/shard_map/all_to_all | solution.py:69
  31.6 6.8 %gather_fusion.5 = bf16[1024]{0:T(1024)(128)(2,1)S(1)} fusion(bf16[1025]{0:T(1024)(128)(2,1)S(1)} %pad_maximum_fusion.1, s32[1024]{0:T(1024)S(1)} %get-tuple-element.33), kind=kCustom, calls=%fused_computation.5 | custom fusion | bytes 8192 | tf_op jit(solution)/shard_map/gather | solution.py:100
  38.5 2.7 gather_fusion.3
  41.2 1.0 concatenate.21
  42.2 5.4 %gather_fusion.4 = bf16[1024,1024]{1,0:T(8,128)(2,1)} fusion(bf16[129,1024]{1,0:T(8,128)(2,1)S(1)} %concatenate.21, s32[1024]{0:T(1024)S(1)} %get-tuple-element.34), kind=kCustom, calls=%fused_computation.4 | custom fusion | bytes 4198400 | tf_op jit(solution)/shard_map/gather | solution.py:101
  47.6 3.4 %fusion = bf16[4,4,64,1024]{3,2,1,0:T(8,128)(2,1)} fusion(bf16[4,4,64,1024]{3,2,1,0:T(8,128)(2,1)} %bitcast.147, f32[4,4,64]{2,1,0:T(4,128)S(1)} %reshape.112), kind=kLoop, calls=%fused_computation.14 | loop fusion | flops 3145728 | bytes 4198400 | tf_op jit(solution)/shard_map/convert_element_type | solution.py:102
  50.9 5.8 %all-to-all-done = bf16[4,4,64,1024]{3,2,1,0:T(8,128)(2,1)} async-done(((bf16[4,4,64,1024]{3,2,1,0:T(8,128)(2,1)}), bf16[4,4,64,1024]{3,2,1,0:T(8,128)(2,1)}, u32[]{:S(2)}, u32[]{:S(2)}) %all-to-all-start) | async-done | bytes 2097184 | tf_op jit(solution)/shard_map/all_to_all | solution.py:69
  56.7 4.5 %all-to-all-start.4 = ((bf16[4,4,64,1024]{3,2,1,0:T(8,128)(2,1)}), bf16[4,4,64,1024]{3,2,1,0:T(8,128)(2,1)}, u32[]{:S(2)}, u32[]{:S(2)}) async-start(bf16[4,4,64,1024]{3,2,1,0:T(8,128)(2,1)} %fusion), calls=%async_computation.4 | async-start | bytes 4194304 | tf_op jit(solution)/shard_map/all_to_all | solution.py:105
  61.4 5.1 %fusion.6 = f32[4,4,64,384]{3,2,1,0:T(8,128)} fusion(bf16[4,1024,384]{2,1,0:T(8,128)(2,1)} %param.15, bf16[4,4,64,1024]{3,2,1,0:T(8,128)(2,1)} %all-to-all-done), kind=kOutput, calls=%fused_computation.21 | convolution fusion | flops 805306368 | bytes 6815744 | tf_op jit(solution)/shard_map/sekd,edf->sekf/dot_general | solution.py:42
  66.5 4.1 %fusion.10 = f32[4,4,64,384]{3,2,1,0:T(8,128)} fusion(bf16[4,1024,384]{2,1,0:T(8,128)(2,1)S(1)} %copy-done.2, bf16[4,4,64,1024]{3,2,1,0:T(8,128)(2,1)} %all-to-all-done), kind=kOutput, calls=%fused_computation.25 | convolution fusion | flops 805306368 | bytes 6815744 | tf_op jit(solution)/shard_map/sekd,edf->sekf/dot_general | solution.py:41
  70.6 16.3 %all-to-all-done.4 = bf16[4,4,64,1024]{3,2,1,0:T(8,128)(2,1)} async-done(((bf16[4,4,64,1024]{3,2,1,0:T(8,128)(2,1)}), bf16[4,4,64,1024]{3,2,1,0:T(8,128)(2,1)}, u32[]{:S(2)}, u32[]{:S(2)}) %all-to-all-start.4) | async-done | bytes 2097184 | tf_op jit(solution)/shard_map/all_to_all | solution.py:105
  86.9 4.2 %fusion.29 = (bf16[4,4,64,384]{3,2,0,1:T(8,128)(2,1)S(1)}, bf16[4,4,64,384]{3,2,0,1:T(8,128)(2,1)S(1)}, bf16[4,4,64,384]{3,2,0,1:T(8,128)(2,1)S(1)}) fusion(f32[4,4,64,384]{3,2,1,0:T(8,128)} %fusion.6, f32[4,4,64,384]{3,2,1,0:T(8,128)} %fusion.10, bf16[4,1024,384]{2,1,0:T(8,128)(2,1)S(1)} %copy-done, bf16[4,4,64,1024]{3,2,1,0:T(8,128)(2,1)} %all-to-all-done.4), kind=kOutput, calls=%fused_computation.43 | convolution fusion | flops 811597824 | bytes 10747904 | tf_op jit(solution)/shard_map/sekd,edf->sekf/dot_general | solution.py:108
  91.2 3.5 %fusion.3 = bf16[1024,1,4,384]{0,3,2,1:T(8,128)(2,1)S(1)} fusion(bf16[4,4,64,384]{3,2,0,1:T(8,128)(2,1)S(1)} %get-tuple-element.28, bf16[4,4,64,1024]{3,2,1,0:T(8,128)(2,1)} %all-to-all-done.4), kind=kOutput, calls=%fused_computation.18 | convolution fusion | flops 806879232 | bytes 6029312 | tf_op jit(solution)/shard_map/sekd,sekf->def/dot_general | solution.py:144
  94.6 2.6 fusion.2
  97.3 2.6 fusion.1
  99.9 4.1 %pad_maximum_fusion = bf16[1024,3,4,384]{0,3,2,1:T(8,128)(2,1)} fusion(bf16[1024,1,4,384]{0,3,2,1:T(8,128)(2,1)S(1)} %fusion.3, bf16[1024,1,4,384]{0,3,2,1:T(8,128)(2,1)S(1)} %fusion.2, bf16[1024,1,4,384]{0,3,2,1:T(8,128)(2,1)S(1)} %fusion.1), kind=kLoop, calls=%fused_computation.9 | loop fusion | flops 9437184 | bytes 18874368 | tf_op jit(solution)/shard_map/concatenate | solution.py:141
  104.0 12.4 %copy.93 = bf16[1024,4608]{1,0:T(8,128)(2,1)} copy(bf16[1024,4608]{0,1:T(8,128)(2,1)} %bitcast.144) | data formatting | bytes 18874368
  116.5 2.4 convert_bitcast_fusion
  118.9 1.7 copy.68
  120.6 4.7 %all-to-all-start.1 = ((bf16[4,4,64,1024]{3,2,1,0:T(8,128)(2,1)}), bf16[4,4,64,1024]{3,2,1,0:T(8,128)(2,1)}, u32[]{:S(2)}, u32[]{:S(2)}) async-start(bf16[4,4,64,1024]{3,2,1,0:T(8,128)(2,1)} %copy.68), calls=%async_computation.1 | async-start | bytes 4194304 | tf_op jit(solution)/shard_map/all_to_all | solution.py:73
  125.3 2.6 fusion.4
  127.9 1.3 fusion.16
  129.2 1.6 copy.74
  130.8 20.3 %all-to-all-done.1 = bf16[4,4,64,1024]{3,2,1,0:T(8,128)(2,1)} async-done(((bf16[4,4,64,1024]{3,2,1,0:T(8,128)(2,1)}), bf16[4,4,64,1024]{3,2,1,0:T(8,128)(2,1)}, u32[]{:S(2)}, u32[]{:S(2)}) %all-to-all-start.1) | async-done | bytes 2097184 | tf_op jit(solution)/shard_map/all_to_all | solution.py:73
  151.1 4.5 %all-to-all-start.5 = ((bf16[4,4,64,1024]{3,2,1,0:T(8,128)(2,1)}), bf16[4,4,64,1024]{3,2,1,0:T(8,128)(2,1)}, u32[]{:S(2)}, u32[]{:S(2)}) async-start(bf16[4,4,64,1024]{3,2,1,0:T(8,128)(2,1)} %copy.74), calls=%async_computation.5 | async-start | bytes 4194304 | tf_op jit(solution)/shard_map/all_to_all | solution.py:122
  155.9 1.2 scatter_custom_fusion.1
  157.1 2.0 concatenate.20
  159.1 5.4 %gather_fusion.1 = bf16[1024,1024]{1,0:T(8,128)(2,1)} fusion(bf16[1025,1024]{1,0:T(8,128)(2,1)S(1)} %concatenate.20, s32[1024]{0:T(1024)S(1)} %broadcast_clamp_fusion), kind=kCustom, calls=%fused_computation.1 | custom fusion | bytes 4198400 | tf_op jit(solution)/shard_map/gather | solution.py:82
  164.5 2.3 fusion.19
  166.8 1.6 gather_fusion.2
  168.4 12.9 %all-to-all-done.5 = bf16[4,4,64,1024]{3,2,1,0:T(8,128)(2,1)} async-done(((bf16[4,4,64,1024]{3,2,1,0:T(8,128)(2,1)}), bf16[4,4,64,1024]{3,2,1,0:T(8,128)(2,1)}, u32[]{:S(2)}, u32[]{:S(2)}) %all-to-all-start.5) | async-done | bytes 2097184 | tf_op jit(solution)/shard_map/all_to_all | solution.py:122
  181.3 6.0 %all-to-all-start.2 = ((bf16[8,16,1024]{2,1,0:T(8,128)(2,1)}), bf16[8,16,1024]{2,1,0:T(8,128)(2,1)S(1)}, u32[]{:S(2)}, u32[]{:S(2)}) async-start(bf16[8,16,1024]{2,1,0:T(8,128)(2,1)} %bitcast.15), calls=%async_computation.2 | async-start | bytes 524288 | tf_op jit(solution)/shard_map/all_to_all | solution.py:92
  187.3 1.8 concatenate.23
  189.0 5.4 %gather_fusion.6 = bf16[1024,1024]{1,0:T(8,128)(2,1)} fusion(bf16[1025,1024]{1,0:T(8,128)(2,1)S(1)} %concatenate.23, s32[1024]{0:T(1024)S(1)} %broadcast_clamp_fusion), kind=kCustom, calls=%fused_computation.6 | custom fusion | bytes 4198400 | tf_op jit(solution)/shard_map/gather | solution.py:128
  194.4 2.3 fusion.17
  196.7 0.8 copy.111
  197.5 7.4 %all-to-all-done.2 = bf16[8,16,1024]{2,1,0:T(8,128)(2,1)S(1)} async-done(((bf16[8,16,1024]{2,1,0:T(8,128)(2,1)}), bf16[8,16,1024]{2,1,0:T(8,128)(2,1)S(1)}, u32[]{:S(2)}, u32[]{:S(2)}) %all-to-all-start.2) | async-done | bytes 262176 | tf_op jit(solution)/shard_map/all_to_all | solution.py:92
  204.9 82.3 %reduce-scatter.4.cloned.1.call-done = bf16[128,4608]{1,0:T(8,128)(2,1)} async-done(((bf16[1024,4608]{1,0:T(8,128)(2,1)}), bf16[128,4608]{1,0:T(8,128)(2,1)}) %reduce-scatter.4.cloned.1.call-update) | async-done | bytes 1179664
  287.1 2.4 copy.94
  289.5 1.5 convert_element_type.70
  291.0 1.5 fusion.41
  292.4 2.4 copy.78
  294.9 2.3 copy.79
  297.1 2.3 copy.80
  (52 shorter events, 3.1 us)
Async XLA Ops:
  7.2 79.8 %copy-start = (bf16[4,1024,384]{2,1,0:T(8,128)(2,1)S(1)}, bf16[4,1024,384]{2,1,0:T(8,128)(2,1)}, u32[]{:S(2)}) copy-start(bf16[4,1024,384]{2,1,0:T(8,128)(2,1)} %param.16) | copy-start | bytes 9437188
  7.2 19.2 %all-to-all-start.3 = ((bf16[8,16,1024]{2,1,0:T(8,128)(2,1)}), bf16[8,16,1024]{2,1,0:T(8,128)(2,1)}, u32[]{:S(2)}, u32[]{:S(2)}) async-start(bf16[8,16,1024]{2,1,0:T(8,128)(2,1)} %bitcast.151), calls=%async_computation.3 | async-start | bytes 524288 | tf_op jit(solution)/shard_map/all_to_all | solution.py:96
  26.3 4.6 %copy-start.10 = (s32[128]{0:T(128)S(1)}, s32[128]{0:T(128)}, u32[]{:S(2)}) copy-start(s32[128]{0:T(128)} %param.13) | copy-start | bytes 1540
  26.3 4.9 %copy-start.9 = (bf16[128,8]{0,1:T(8,128)(2,1)S(1)}, bf16[128,8]{0,1:T(8,128)(2,1)}, u32[]{:S(2)}) copy-start(bf16[128,8]{0,1:T(8,128)(2,1)} %param.12) | copy-start | bytes 6148
  26.4 30.4 %all-to-all-start = ((bf16[4,4,64,1024]{3,2,1,0:T(8,128)(2,1)}), bf16[4,4,64,1024]{3,2,1,0:T(8,128)(2,1)}, u32[]{:S(2)}, u32[]{:S(2)}) async-start(bf16[4,4,64,1024]{3,2,1,0:T(8,128)(2,1)} %bitcast.146), calls=%async_computation | async-start | bytes 4194304 | tf_op jit(solution)/shard_map/all_to_all | solution.py:69
  56.7 30.2 %all-to-all-start.4 = ((bf16[4,4,64,1024]{3,2,1,0:T(8,128)(2,1)}), bf16[4,4,64,1024]{3,2,1,0:T(8,128)(2,1)}, u32[]{:S(2)}, u32[]{:S(2)}) async-start(bf16[4,4,64,1024]{3,2,1,0:T(8,128)(2,1)} %fusion), calls=%async_computation.4 | async-start | bytes 4194304 | tf_op jit(solution)/shard_map/all_to_all | solution.py:105
  61.2 225.9 %reduce-scatter.4.cloned.1.call-start = ((), (), s32[]{:S(2)}) async-start(), calls=%async_computation.7 | async-start | bytes 10616832
  61.4 5.1 %copy-start.2 = (bf16[4,1024,384]{2,1,0:T(8,128)(2,1)S(1)}, bf16[4,1024,384]{2,1,0:T(8,128)(2,1)}, u32[]{:S(2)}) copy-start(bf16[4,1024,384]{2,1,0:T(8,128)(2,1)} %param.14) | copy-start | bytes 9437188
  91.1 3.5 %copy-start.5 = (bf16[4,4,64,384]{3,2,0,1:T(8,128)(2,1)}, bf16[4,4,64,384]{3,2,0,1:T(8,128)(2,1)S(1)}, u32[]{:S(2)}) copy-start(bf16[4,4,64,384]{3,2,0,1:T(8,128)(2,1)S(1)} %get-tuple-element.28) | copy-start | bytes 2359300
  91.1 3.5 %copy-start.8 = (bf16[4,4,64,384]{3,2,0,1:T(8,128)(2,1)}, bf16[4,4,64,384]{3,2,0,1:T(8,128)(2,1)S(1)}, u32[]{:S(2)}) copy-start(bf16[4,4,64,384]{3,2,0,1:T(8,128)(2,1)S(1)} %get-tuple-element.29) | copy-start | bytes 2359300
  91.2 6.1 %copy-start.6 = (bf16[4,4,64,384]{3,2,0,1:T(8,128)(2,1)}, bf16[4,4,64,384]{3,2,0,1:T(8,128)(2,1)S(1)}, u32[]{:S(2)}) copy-start(bf16[4,4,64,384]{3,2,0,1:T(8,128)(2,1)S(1)} %get-tuple-element.27) | copy-start | bytes 2359300
  120.6 4.7 %copy-start.4 = (bf16[4,1024,384]{2,1,0:T(8,128)(2,1)S(1)}, bf16[4,1024,384]{2,1,0:T(8,128)(2,1)}, u32[]{:S(2)}) copy-start(bf16[4,1024,384]{2,1,0:T(8,128)(2,1)} %param.15) | copy-start | bytes 9437188
  120.6 30.5 %all-to-all-start.1 = ((bf16[4,4,64,1024]{3,2,1,0:T(8,128)(2,1)}), bf16[4,4,64,1024]{3,2,1,0:T(8,128)(2,1)}, u32[]{:S(2)}, u32[]{:S(2)}) async-start(bf16[4,4,64,1024]{3,2,1,0:T(8,128)(2,1)} %copy.68), calls=%async_computation.1 | async-start | bytes 4194304 | tf_op jit(solution)/shard_map/all_to_all | solution.py:73
  125.3 2.6 copy-start.3
  125.3 2.6 copy-start.7
  151.1 30.2 %all-to-all-start.5 = ((bf16[4,4,64,1024]{3,2,1,0:T(8,128)(2,1)}), bf16[4,4,64,1024]{3,2,1,0:T(8,128)(2,1)}, u32[]{:S(2)}, u32[]{:S(2)}) async-start(bf16[4,4,64,1024]{3,2,1,0:T(8,128)(2,1)} %copy.74), calls=%async_computation.5 | async-start | bytes 4194304 | tf_op jit(solution)/shard_map/all_to_all | solution.py:122
  181.3 23.6 %all-to-all-start.2 = ((bf16[8,16,1024]{2,1,0:T(8,128)(2,1)}), bf16[8,16,1024]{2,1,0:T(8,128)(2,1)S(1)}, u32[]{:S(2)}, u32[]{:S(2)}) async-start(bf16[8,16,1024]{2,1,0:T(8,128)(2,1)} %bitcast.15), calls=%async_computation.2 | async-start | bytes 524288 | tf_op jit(solution)/shard_map/all_to_all | solution.py:92
  292.4 7.7 %copy-start.1 = (bf16[4,1024,384]{2,1,0:T(8,128)(2,1)S(1)}, bf16[4,1024,384]{2,1,0:T(8,128)(2,1)}, u32[]{:S(2)}) copy-start(bf16[4,1024,384]{2,1,0:T(8,128)(2,1)} %param.16) | copy-start | bytes 9437188
Sparse Core Ops, SparseCore 0:
  116.6 170.4 reduce-scatter.3
where the time goes:
time: 309 us; the launch traced here: 307 us
  waiting for transfers between devices  145 us (47%)
  local copies, waits for them, and re-layouts  71.4 us (23%)
  matrix products  32.8 us (11%)
  starting transfers between devices  32 us (10%)
  between operations  14.4 us (5%)
  other arithmetic  11.4 us (4%)
    unnamed x2, waiting for transfers between devices  82.3 us
    unnamed x30, local copies, waits for them, and re-layouts  22.8 us
    all_to_all x1, waiting for transfers between devices, on_device(): lax.all_to_all(outputs, 'expert', split_axis=0, concat_axis=0, tiled=True)  20.3 us
    all_to_all x1, waiting for transfers between devices, on_device(): lax.all_to_all(sending.reshape(slot_shape), 'expert', split_axis=0, conca...  16.3 us
    all_to_all x1, waiting for transfers between devices, on_device(): lax.all_to_all(grad_in.astype(jnp.bfloat16), 'expert', split_axis=0, conc...  12.9 us
    all_to_all x1, starting transfers between devices, on_device(): lax.all_to_all(owner_grads, 'dp', split_axis=0, concat_axis=0, tiled=True)  7.53 us
    all_to_all x1, waiting for transfers between devices, on_device(): lax.all_to_all(owner_rows, 'dp', split_axis=0, concat_axis=0, tiled=True)  7.37 us
    gather x1, local copies, waits for them, and re-layouts, on_device(): weight_slots = padded(combine_weight.reshape(-1))[source_table]  6.8 us
  transfers between devices with their start and end apart: 7, of which 6 were waited for; matrix products, arithmetic and copies ran while one was open for 24% of the time, Pallas kernels for 0%

commit v1 on v0

v1 whole, which is shorter than its diff:
```python
import functools

import jax
import jax.numpy as jnp
from jax import lax
from jax.experimental import pallas as pl
from jax.experimental.pallas import tpu as pltpu
from jax.sharding import PartitionSpec as P

EXPERTS = 16
CAP = 64
MESH = pl.DeviceIdType.MESH
BF = jnp.bfloat16
F32 = jnp.float32
VMEM = pl.BlockSpec(memory_space=pltpu.VMEM)


def remote(src, dst, send, recv, where):
    return pltpu.make_async_remote_copy(
        src_ref=src, dst_ref=dst, send_sem=send, recv_sem=recv, device_id=where, device_id_type=MESH
    )


def greet(experts, data):
    c, s = lax.axis_index("expert"), lax.axis_index("dp")
    barrier = pltpu.get_barrier_semaphore()
    for k in range(1, experts):
        pl.semaphore_signal(
            barrier, inc=1, device_id={"expert": lax.rem(c + k, experts)}, device_id_type=MESH
        )
    for k in range(1, data):
        pl.semaphore_signal(
            barrier, inc=1, device_id={"dp": lax.rem(s + k, data)}, device_id_type=MESH
        )
    pl.semaphore_wait(barrier, experts + data - 2)


def gather_kernel(
    experts, data, tok, meta, gt, tok_all, meta_all, up_all, gs, gr, ts, tr, ms, mr, us, ur
):
    c, s = lax.axis_index("expert"), lax.axis_index("dp")
    greet(experts, data)
    grads, rows, metas, ups = [], [], [], []
    for k in range(1, data):
        peer = lax.rem(s + k, data)
        grads.append(
            remote(gt.at[peer], up_all.at[c, s], gs.at[k - 1], gr.at[k - 1], {"dp": peer})
        )
        grads[-1].start()
    for k in range(1, experts):
        peer = {"expert": lax.rem(c + k, experts)}
        metas.append(remote(meta, meta_all.at[c], ms.at[k - 1], mr.at[k - 1], peer))
        metas[-1].start()
        rows.append(remote(tok, tok_all.at[c], ts.at[k - 1], tr.at[k - 1], peer))
        rows[-1].start()
    tok_all[c] = tok[...]
    meta_all[c] = meta[...]
    up_all[c, s] = gt[s]
    for copy in grads:
        copy.wait_recv()
    for k in range(1, experts):
        peer = {"expert": lax.rem(c + k, experts)}
        ups.append(remote(up_all.at[c], up_all.at[c], us.at[k - 1], ur.at[k - 1], peer))
        ups[-1].start()
    for copy in grads:
        copy.wait_send()
    for copy in metas + rows + ups:
        copy.wait()


def gather_all(tokens, meta, owner_grads):
    experts, data = lax.axis_size("expert"), lax.axis_size("dp")
    dma = pltpu.SemaphoreType.DMA
    return pl.pallas_call(
        functools.partial(gather_kernel, experts, data),
        out_shape=(
            jax.ShapeDtypeStruct((experts,) + tokens.shape, BF),
            jax.ShapeDtypeStruct((experts,) + meta.shape, F32),
            jax.ShapeDtypeStruct((experts,) + owner_grads.shape, BF),
        ),
        in_specs=[VMEM] * 3,
        out_specs=(VMEM,) * 3,
        scratch_shapes=[dma((data - 1,))] * 2 + [dma((experts - 1,))] * 6,
        compiler_params=pltpu.CompilerParams(collective_id=0, has_side_effects=True),
    )(tokens, meta, owner_grads)


def dot(a, b, ca, cb):
    return lax.dot_general(a, b, (((ca,), (cb,)), ((), ())), preferred_element_type=F32)


def compute_kernel(
    local, tok, meta, up, gw, uw, dw, mixed, gtok, parts, dmat, cmat, xs, gs, outs, gins
):
    e = pl.program_id(0)
    blocks, rows, width = tok.shape
    slots = local * CAP
    pairs = meta.shape[1] // 3

    @pl.when(e == 0)
    def _():
        base = (lax.axis_index("expert") * slots).astype(F32)
        want = lax.broadcasted_iota(jnp.int32, (slots, rows), 0).astype(F32) + base
        for b in range(blocks):
            hit = jnp.zeros((slots, rows), F32)
            held = jnp.zeros((slots, rows), F32)
            for k in range(pairs):
                hit = jnp.where(meta[b, k : k + 1, :] == want, 1.0, hit)
                held = jnp.where(
                    meta[b, pairs + k : pairs + k + 1, :] == want,
                    meta[b, 2 * pairs + k : 2 * pairs + k + 1, :],
                    held,
                )
            dmat[b] = hit.astype(BF)
            cmat[b] = held.astype(BF)
            xs[b] = dot(dmat[b], tok[b], 1, 0).astype(BF)
            gs[b] = dot(cmat[b], up[b], 1, 0).astype(BF)

    here = pl.ds(pl.multiple_of(e * CAP, CAP), CAP)
    x = xs[:, here, :].reshape(blocks * CAP, width)
    g = gs[:, here, :].reshape(blocks * CAP, width)
    gate = dot(x, gw[0], 1, 0)
    upv = dot(x, uw[0], 1, 0)
    sig = 1.0 / (1.0 + jnp.exp(-gate))
    hidden = (gate * sig * upv).astype(BF)
    gh = dot(g, dw[0], 1, 0)
    gu = (gh * gate * sig).astype(BF)
    gg = (gh * upv * sig * (1.0 + gate * (1.0 - sig))).astype(BF)
    outs[:, here, :] = dot(hidden, dw[0], 1, 1).astype(BF).reshape(blocks, CAP, width)
    gin = dot(gg, gw[0], 1, 1) + dot(gu, uw[0], 1, 1)
    gins[:, here, :] = gin.astype(BF).reshape(blocks, CAP, width)
    parts[0, 0] = dot(x, gg, 0, 0).astype(BF)
    parts[1, 0] = dot(x, gu, 0, 0).astype(BF)
    parts[2, 0] = dot(g, hidden, 0, 0).astype(BF)

    @pl.when(e == local - 1)
    def _():
        for b in range(blocks):
            mixed[b] = dot(cmat[b], outs[b], 0, 0).astype(BF)
            gtok[b] = dot(dmat[b], gins[b], 0, 0).astype(BF)


def compute_all(tok, meta, up, gate_weight, up_weight, down_weight):
    local, width, ff = gate_weight.shape
    blocks, rows, _ = tok.shape
    slots = local * CAP
    whole = lambda shape: pl.BlockSpec(shape, lambda e: (0,) * len(shape))
    weight = pl.BlockSpec((1, width, ff), lambda e: (e, 0, 0))
    return pl.pallas_call(
        functools.partial(compute_kernel, local),
        grid=(local,),
        out_shape=(
            jax.ShapeDtypeStruct((blocks, rows, width), BF),
            jax.ShapeDtypeStruct((blocks, rows, width), BF),
            jax.ShapeDtypeStruct((3, local, width, ff), BF),
        ),
        in_specs=[whole(tok.shape), whole(meta.shape), whole(up.shape), weight, weight, weight],
        out_specs=(
            whole((blocks, rows, width)),
            whole((blocks, rows, width)),
            pl.BlockSpec((3, 1, width, ff), lambda e: (0, e, 0, 0)),
        ),
        scratch_shapes=[
            pltpu.VMEM((blocks, slots, rows), BF),
            pltpu.VMEM((blocks, slots, rows), BF),
            pltpu.VMEM((blocks, slots, width), BF),
            pltpu.VMEM((blocks, slots, width), BF),
            pltpu.VMEM((blocks, slots, width), BF),
            pltpu.VMEM((blocks, slots, width), BF),
        ],
        compiler_params=pltpu.CompilerParams(vmem_limit_bytes=56 * 2**20),
    )(tok, meta, up, gate_weight, up_weight, down_weight)


def reduce_kernel(
    experts, nz, nx, part, mixed, gtok, total, talk, grads,
    xrecv, xsum, below, above, mrecv, grecv, msum,
    xss, xrs, bss, brs, ass, ars, mss, mrs, gss, grs, tss, trs,
):
    data = nz * nx
    c, s = lax.axis_index("expert"), lax.axis_index("dp")
    z, x = lax.div(s, nx), lax.rem(s, nx)
    chunks = part.shape[0]
    greet(experts, data)

    def xcopy(i, k):
        px = lax.rem(x + k, nx)
        return remote(
            part.at[i, :, px], xrecv.at[k - 1, i], xss.at[k - 1, i], xrs.at[k - 1, i],
            {"dp": z * nx + px},
        )

    def upcopy(i, d):
        return remote(
            xsum.at[i, d], below.at[i, d], bss.at[i, d], brs.at[i, d], {"dp": lax.rem(s + nx, data)}
        )

    def downcopy(i, d):
        return remote(
            xsum.at[i, d], above.at[i, d], ass.at[i, d], ars.at[i, d],
            {"dp": lax.rem(s + data - nx, data)},
        )

    @pl.loop(0, chunks)
    def _(i):
        for k in range(1, nx):
            xcopy(i, k).start()

    backs, talks = [], []
    for k in range(1, experts):
        peer = lax.rem(c + k, experts)
        backs.append(
            remote(mixed.at[peer], mrecv.at[k - 1], mss.at[k - 1], mrs.at[k - 1], {"expert": peer})
        )
        backs[-1].start()
    grad_backs = []
    for k in range(1, experts):
        peer = lax.rem(c + k, experts)
        grad_backs.append(
            remote(gtok.at[peer], grecv.at[k - 1], gss.at[k - 1], grs.at[k - 1], {"expert": peer})
        )
        grad_backs[-1].start()

    def step(i):
        @pl.when(i < chunks)
        def _():
            for k in range(1, nx):
                xcopy(i, k).wait_recv()
            for d in range(nz):
                held = part[i, d, x].astype(F32)
                for k in range(1, nx):
                    held = held + xrecv[k - 1, i, d].astype(F32)
                xsum[i, d] = held.astype(BF)

        rise = i - z

        @pl.when((rise >= 0) & (rise < chunks))
        def _():
            for d in range(1, nz):
                @pl.when((z > 0) & (z < d))
                def _():
                    upcopy(rise, d).wait_recv()
                    xsum[rise, d] = (
                        xsum[rise, d].astype(F32) + below[rise, d].astype(F32)
                    ).astype(BF)

                @pl.when(z < d)
                def _():
                    upcopy(rise, d).start()

        fall = i - (nz - 1 - z)

        @pl.when((fall >= 0) & (fall < chunks))
        def _():
            for d in range(nz - 1):
                @pl.when((z < nz - 1) & (z > d))
                def _():
                    downcopy(fall, d).wait_recv()
                    xsum[fall, d] = (
                        xsum[fall, d].astype(F32) + above[fall, d].astype(F32)
                    ).astype(BF)

                @pl.when(z > d)
                def _():
                    downcopy(fall, d).start()

        last = i - (nz - 1)

        @pl.when(last >= 0)
        def _():
            total[last] = xsum[last, z].astype(F32) * (1.0 / data)

            @pl.when(z > 0)
            def _():
                upcopy(last, z).wait_recv()
                total[last] += below[last, z].astype(F32) * (1.0 / data)

            @pl.when(z < nz - 1)
            def _():
                downcopy(last, z).wait_recv()
                total[last] += above[last, z].astype(F32) * (1.0 / data)

    early = min(2, chunks)
    pl.loop(0, early)(step)

    for copy in backs:
        copy.wait_recv()
    held = mixed[c].astype(F32)
    for k in range(experts - 1):
        held = held + mrecv[k].astype(F32)
    msum[...] = held.astype(BF)
    for k in range(1, data):
        peer = lax.rem(s + k, data)
        talks.append(remote(msum.at[peer], talk.at[s], tss.at[k - 1], trs.at[k - 1], {"dp": peer}))
        talks[-1].start()
    talk[s] = msum[s]
    for copy in grad_backs:
        copy.wait_recv()
    held = gtok[c].astype(F32)
    for k in range(experts - 1):
        held = held + grecv[k].astype(F32)
    grads[...] = held.astype(BF)

    pl.loop(early, chunks + nz - 1)(step)

    for copy in backs + grad_backs:
        copy.wait_send()
    for copy in talks:
        copy.wait()

    @pl.loop(0, chunks)
    def _(i):
        for k in range(1, nx):
            xcopy(i, k).wait_send()
        for d in range(nz):
            @pl.when(d > z)
            def _():
                upcopy(i, d).wait_send()

            @pl.when(d < z)
            def _():
                downcopy(i, d).wait_send()


def reduce_all(parts, mixed, gtok):
    experts, data = lax.axis_size("expert"), lax.axis_size("dp")
    nx = 1 << ((data.bit_length() - 1) // 2)
    nz = data // nx
    three, local, width, ff = parts.shape
    chunks, rows = three * local, width // data
    blocks, tok_rows, _ = mixed.shape
    per_owner = tok_rows // data
    parts = parts.reshape(chunks, nz, nx, rows, ff)
    mixed = mixed.reshape(blocks, data, per_owner, width)
    dma = pltpu.SemaphoreType.DMA
    return pl.pallas_call(
        functools.partial(reduce_kernel, experts, nz, nx),
        out_shape=(
            jax.ShapeDtypeStruct((chunks, rows, ff), F32),
            jax.ShapeDtypeStruct((data, per_owner, width), BF),
            jax.ShapeDtypeStruct((tok_rows, width), BF),
        ),
        in_specs=[VMEM] * 3,
        out_specs=(VMEM,) * 3,
        scratch_shapes=[
            pltpu.VMEM((nx - 1, chunks, nz, rows, ff), BF),
            pltpu.VMEM((chunks, nz, rows, ff), BF),
            pltpu.VMEM((chunks, nz, rows, ff), BF),
            pltpu.VMEM((chunks, nz, rows, ff), BF),
            pltpu.VMEM((experts - 1, data, per_owner, width), BF),
            pltpu.VMEM((experts - 1, tok_rows, width), BF),
            pltpu.VMEM((data, per_owner, width), BF),
            dma((nx - 1, chunks)),
            dma((nx - 1, chunks)),
            dma((chunks, nz)),
            dma((chunks, nz)),
            dma((chunks, nz)),
            dma((chunks, nz)),
            dma((experts - 1,)),
            dma((experts - 1,)),
            dma((experts - 1,)),
            dma((experts - 1,)),
            dma((data - 1,)),
            dma((data - 1,)),
        ],
        compiler_params=pltpu.CompilerParams(
            collective_id=1, has_side_effects=True, vmem_limit_bytes=56 * 2**20
        ),
    )(parts, mixed, gtok)


def on_device(
    tokens,
    expert_ids,
    slot_index,
    combine_weight,
    talker_owner,
    gate_weight,
    up_weight,
    down_weight,
    grad_talker,
):
    data = lax.axis_size("dp")
    rows, width = tokens.shape
    per_owner = rows // data
    local = gate_weight.shape[0]
    order = jnp.arange(rows, dtype=jnp.int32)
    same = (talker_owner[:, None] == talker_owner[None, :]) & (order[:, None] < order[None, :])
    owner_slot = talker_owner * per_owner + jnp.sum(same.astype(jnp.int32), axis=0)
    position = jnp.where(slot_index >= 0, expert_ids * CAP + slot_index, -1).astype(F32).T
    weight = combine_weight.astype(F32).T
    pick = owner_slot[None, :] == order[:, None]
    moved = jnp.sum(
        jnp.where(pick[None], jnp.concatenate([position, weight], 0)[:, None, :], 0.0), axis=2
    )
    meta = jnp.concatenate([position, moved], 0)
    tok_all, meta_all, up_all = gather_all(
        tokens, meta, grad_talker.reshape(data, per_owner, width)
    )
    mixed, gtok, parts = compute_all(
        tok_all,
        meta_all,
        up_all.reshape(tok_all.shape),
        gate_weight,
        up_weight,
        down_weight,
    )
    total, talk, grad_tokens = reduce_all(parts, mixed, gtok)
    return (
        talk.reshape(rows, width),
        grad_tokens,
        total[:local],
        total[local : 2 * local],
        total[2 * local :],
    )


def solution(mesh):
    placed = (
        P(("dp", "expert"), None),
        P(("dp", "expert"), None),
        P(("dp", "expert"), None),
        P(("dp", "expert"), None),
        P(("dp", "expert")),
        P("expert", None, None),
        P("expert", None, None),
        P("expert", None, None),
        P(("dp", "expert"), None),
    )
    return jax.shard_map(
        on_device,
        mesh=mesh,
        in_specs=placed,
        out_specs=(
            P(("dp", "expert"), None),
            P(("dp", "expert"), None),
            P("expert", "dp", None),
            P("expert", "dp", None),
            P("expert", "dp", None),
        ),
        check_vma=False,
    )
```

time: 309 us -> 189 us (0.61)
  Pallas kernels: 0 us -> 179 us
  waiting for transfers between devices: 145 us -> 0 us
  local copies, waits for them, and re-layouts: 71.4 us -> 4.53 us
  matrix products: 32.8 us -> 0 us
  starting transfers between devices: 32 us -> 0 us
  between operations: 14.4 us -> 0.68 us
  other arithmetic: 11.4 us -> 3.85 us
    pallas_call x0 -> x3, Pallas kernels: none -> 179 us  [the longest x1 130 us: reduce_all(): pl.pallas_call(functools.partial(reduce_kernel, experts, nz, nx), out_sha...]
    unnamed x2 -> x0, waiting for transfers between devices: 82.3 us -> none
    all_to_all x6 -> x0, waiting for transfers between devices: 62.7 us -> none  [the longest x1 20.3 us: on_device(): lax.all_to_all(outputs, 'expert', split_axis=0, concat_axis=0, tiled=True)]
    dot_general x11 -> x0, matrix products: 32.8 us -> none  [the longest x1 5.06 us: expert_forward(): jnp.einsum('sekd,edf->sekf', inputs, up_weight, preferred_element_type=jn...]
    gather x7 -> x0, local copies, waits for them, and re-layouts: 32.6 us -> none  [the longest x1 6.8 us: on_device(): weight_slots = padded(combine_weight.reshape(-1))[source_table]]
    all_to_all x6 -> x0, starting transfers between devices: 31.8 us -> none  [the longest x1 7.53 us: on_device(): lax.all_to_all(owner_grads, 'dp', split_axis=0, concat_axis=0, tiled=True)]
    unnamed x30 -> x6, local copies, waits for them, and re-layouts: 22.8 us -> 1.41 us
    concatenate x4 -> x0, local copies, waits for them, and re-layouts: 5.67 us -> none  [padded(): jnp.concatenate([values, jnp.zeros((1,) + values.shape[1:], values.dtype)...]
  transfers between devices with their start and end apart: 7 -> 0, of which waited for: 6 -> 0; matrix products, arithmetic and copies ran while one was open for 24% -> 0% of each run, Pallas kernels for 0% -> 0%
where the time goes in v1:
time: 189 us; the launch traced here: 188 us
  Pallas kernels  179 us (95%)
  local copies, waits for them, and re-layouts  4.53 us (2%)
  other arithmetic  3.85 us (2%)
    pallas_call x1, Pallas kernels, reduce_all(): pl.pallas_call(functools.partial(reduce_kernel, experts, nz, nx), out_sha...  130 us
    pallas_call x1, Pallas kernels, gather_all(): pl.pallas_call(functools.partial(gather_kernel, experts, data), out_shape...  31.6 us
    pallas_call x1, Pallas kernels, compute_all(): pl.pallas_call(functools.partial(compute_kernel, local), grid=(local,), o...  17.5 us

profile of v1, /device:TPU:0, one launch (start us, length us, event | category | flops | bytes accessed | tf_op | source)
XLA Modules:
  0.0 188.4 jit_solution(12153586086660021517)
XLA Ops:
  0.6 0.8 convert_reduce_fusion
  1.5 0.7 multiply_add_fusion
  2.1 0.7 convert_bitcast_fusion.1
  2.8 0.7 convert_bitcast_fusion
  3.5 0.3 select_reduce_fusion
  3.9 0.6 pad_maximum_fusion.meta
  4.5 31.6 %shard_map.128 = (bf16[4,128,1024]{2,1,0:T(8,128)(2,1)}, f32[4,24,128]{2,1,0:T(8,128)}, bf16[4,8,16,1024]{3,2,1,0:T(8,128)(2,1)}) custom-call(bf16[128,1024]{1,0:T(8,128)(2,1)} %tok.1, f32[24,128]{1,0:T(8,128)} %pad_maximum_fusion.meta, bf16[8,16,1024]{2,1,0:T(8,128)(2,1)} %bitcast.12), custom_call_target="tpu_custom_call" | custom-call | tf_op jit(solution)/shard_map/pallas_call | solution.py:74
  36.1 17.5 %shard_map.129 = (bf16[4,128,1024]{2,1,0:T(8,128)(2,1)}, bf16[4,128,1024]{2,1,0:T(8,128)(2,1)}, bf16[3,4,1024,384]{3,2,1,0:T(8,128)(2,1)}) custom-call(bf16[4,128,1024]{2,1,0:T(8,128)(2,1)} %get-tuple-element.14.tok, f32[4,24,128]{2,1,0:T(8,128)} %get-tuple-element.15.meta, bf16[4,128,1024]{2,1,0:T(8,128)(2,1)} %bitcast.11, bf16[4,1024,384]{2,1,0:T(8,128)(2,1)} %gw.1, ...), custom_call_target="tpu_custom_call" | custom-call | tf_op jit(solution)/shard_map/pallas_call | solution.py:149
  53.6 130.3 %shard_map.130 = (f32[12,128,384]{2,1,0:T(8,128)}, bf16[8,16,1024]{2,1,0:T(8,128)(2,1)}, bf16[128,1024]{1,0:T(8,128)(2,1)}) custom-call(bf16[12,4,2,128,384]{4,3,2,1,0:T(8,128)(2,1)} %bitcast.9, bf16[4,8,16,1024]{3,2,1,0:T(8,128)(2,1)} %bitcast.10, bf16[4,128,1024]{2,1,0:T(8,128)(2,1)} %get-tuple-element.19.gtok), custom_call_target="tpu_custom_call" | custom-call | tf_op jit(solution)/shard_map/pallas_call | solution.py:336
  183.9 0.0 copy-start.1
  183.9 0.0 copy-start
  183.9 3.1 %fusion.1 = (f32[4,128,384]{2,1,0:T(8,128)}, f32[4,128,384]{2,1,0:T(8,128)}, f32[4,128,384]{2,1,0:T(8,128)}) fusion(f32[12,128,384]{2,1,0:T(8,128)} %get-tuple-element.22), kind=kLoop, calls=%fused_computation.10 | loop fusion | bytes 4718592 | tf_op jit(solution)/shard_map/slice | solution.py:414
  187.0 0.0 copy-done.1
  187.0 0.7 copy.16
  187.7 0.0 copy-done
  187.7 0.7 copy.17
  (2 shorter events, 0.0 us)
Async XLA Ops:
  183.9 3.1 %copy-start.1 = (bf16[8,16,1024]{2,1,0:T(8,128)(2,1)S(1)}, bf16[8,16,1024]{2,1,0:T(8,128)(2,1)}, u32[]{:S(2)}) copy-start(bf16[8,16,1024]{2,1,0:T(8,128)(2,1)} %get-tuple-element.20) | copy-start | bytes 786436
  183.9 3.8 %copy-start = (bf16[128,1024]{1,0:T(8,128)(2,1)S(1)}, bf16[128,1024]{1,0:T(8,128)(2,1)}, u32[]{:S(2)}) copy-start(bf16[128,1024]{1,0:T(8,128)(2,1)} %get-tuple-element.32) | copy-start | bytes 786436

commit v2 on v1

v2 whole, which is shorter than its diff:
```python
import functools

import jax
import jax.numpy as jnp
from jax import lax
from jax.experimental import pallas as pl
from jax.experimental.pallas import tpu as pltpu
from jax.sharding import PartitionSpec as P

EXPERTS = 16
CAP = 64
MESH = pl.DeviceIdType.MESH
BF = jnp.bfloat16
F32 = jnp.float32
VMEM = pl.BlockSpec(memory_space=pltpu.VMEM)


def remote(src, dst, send, recv, where):
    return pltpu.make_async_remote_copy(
        src_ref=src, dst_ref=dst, send_sem=send, recv_sem=recv, device_id=where, device_id_type=MESH
    )


def greet(experts, data):
    c, s = lax.axis_index("expert"), lax.axis_index("dp")
    barrier = pltpu.get_barrier_semaphore()
    for k in range(1, experts):
        pl.semaphore_signal(
            barrier, inc=1, device_id={"expert": lax.rem(c + k, experts)}, device_id_type=MESH
        )
    for k in range(1, data):
        pl.semaphore_signal(
            barrier, inc=1, device_id={"dp": lax.rem(s + k, data)}, device_id_type=MESH
        )
    pl.semaphore_wait(barrier, experts + data - 2)


def dot(a, b, ca, cb):
    return lax.dot_general(a, b, (((ca,), (cb,)), ((), ())), preferred_element_type=F32)


def layer_kernel(
    experts, nz, nx, tok, meta, gt, gate_hbm, up_hbm, down_hbm,
    out_gate, out_up, out_down, talk, grads,
    tok_all, meta_all, up_all, gw, uw, dw, dmat, cmat, xs, gs, outs, gins, gates, ups, hid,
    mixed, gtok, part, xrecv, line, mrecv, grecv, msum, acc,
    wsem, gs_s, gr_s, ts_s, tr_s, fs_s, fr_s, ms_s, mr_s, us_s, ur_s, vs_s, vr_s,
    xs_s, xr_s, bs_s, br_s, as_s, ar_s, bks, bkr, gks, gkr, tks, tkr,
):
    data = nz * nx
    c, s = lax.axis_index("expert"), lax.axis_index("dp")
    z, x = lax.div(s, nx), lax.rem(s, nx)
    sibling = c + 1 - 2 * lax.rem(c, 2)
    half = experts // 2
    local, width, ff = gw.shape
    blocks, rows, _ = tok_all.shape
    slots = local * CAP
    pairs = meta.shape[0] // 3
    chunks = 3 * local

    loads = [
        pltpu.make_async_copy(gate_hbm, gw, wsem.at[0]),
        pltpu.make_async_copy(up_hbm, uw, wsem.at[1]),
        pltpu.make_async_copy(down_hbm, dw, wsem.at[2]),
    ]
    for copy in loads:
        copy.start()
    greet(experts, data)

    def shared(src, buf, send, recv):
        copies = []
        for k in range(1, half):
            peer = lax.rem(c + 2 * k, experts)
            copies.append(remote(src, buf.at[c], send.at[k], recv.at[k], {"expert": peer}))
        copies.append(remote(src, buf.at[c], send.at[0], recv.at[0], {"expert": sibling}))
        for copy in copies:
            copy.start()
        return copies

    def passed(copies, buf, send, recv):
        handed = []
        for k in range(1, half):
            copies[k - 1].wait_recv()
            came = lax.rem(c + experts - 2 * k, experts)
            handed.append(
                remote(
                    buf.at[came], buf.at[came], send.at[k - 1], recv.at[k - 1], {"expert": sibling}
                )
            )
            handed[-1].start()
        return handed

    def arrived(copies, handed):
        copies[-1].wait_recv()
        for copy in handed:
            copy.wait_recv()

    owner_grads, metas = [], []
    for k in range(1, data):
        peer = lax.rem(s + k, data)
        owner_grads.append(
            remote(gt.at[peer], up_all.at[c, s], gs_s.at[k - 1], gr_s.at[k - 1], {"dp": peer})
        )
        owner_grads[-1].start()
    for k in range(1, experts):
        peer = {"expert": lax.rem(c + k, experts)}
        metas.append(remote(meta, meta_all.at[c], ms_s.at[k - 1], mr_s.at[k - 1], peer))
        metas[-1].start()
    tok_sent = shared(tok, tok_all, ts_s, tr_s)
    tok_all[c] = tok[...]
    meta_all[c] = meta[...]
    up_all[c, s] = gt[s]
    for copy in owner_grads:
        copy.wait_recv()
    up_sent = shared(up_all.at[c], up_all, us_s, ur_s)
    tok_passed = passed(tok_sent, tok_all, fs_s, fr_s)

    for copy in metas:
        copy.wait_recv()
    base = (c * slots).astype(F32)
    want = lax.broadcasted_iota(jnp.int32, (slots, rows), 0).astype(F32) + base

    @pl.loop(0, blocks)
    def _(b):
        hit = jnp.zeros((slots, rows), F32)
        held = jnp.zeros((slots, rows), F32)
        for k in range(pairs):
            hit = jnp.where(meta_all[b, k : k + 1, :] == want, 1.0, hit)
            held = jnp.where(
                meta_all[b, pairs + k : pairs + k + 1, :] == want,
                meta_all[b, 2 * pairs + k : 2 * pairs + k + 1, :],
                held,
            )
        dmat[b] = hit.astype(BF)
        cmat[b] = held.astype(BF)

    arrived(tok_sent, tok_passed)

    @pl.loop(0, blocks)
    def _(b):
        xs[b] = dot(dmat[b], tok_all[b], 1, 0).astype(BF)

    up_passed = passed(up_sent, up_all, vs_s, vr_s)
    for copy in loads:
        copy.wait()

    def slot_rows(e):
        return pl.ds(pl.multiple_of(e * CAP, CAP), CAP)

    @pl.loop(0, local)
    def _(e):
        rows_x = xs[:, slot_rows(e), :].reshape(blocks * CAP, width)
        gate = dot(rows_x, gw[e], 1, 0)
        upv = dot(rows_x, uw[e], 1, 0)
        hidden = (gate * (1.0 / (1.0 + jnp.exp(-gate))) * upv).astype(BF)
        gates[e] = gate
        ups[e] = upv
        hid[e] = hidden

    arrived(up_sent, up_passed)

    @pl.loop(0, blocks)
    def _(b):
        gs[b] = dot(cmat[b], up_all[b].reshape(rows, width), 1, 0).astype(BF)

    def xcopy(i, k):
        px = lax.rem(x + k, nx)
        return remote(
            part.at[i, :, px], xrecv.at[k - 1, i], xs_s.at[k - 1, i], xr_s.at[k - 1, i],
            {"dp": z * nx + px},
        )

    def upcopy(i, d):
        return remote(
            xrecv.at[0, i, d], line.at[i, d + 1], bs_s.at[i, d], br_s.at[i, d],
            {"dp": lax.rem(s + nx, data)},
        )

    def downcopy(i, d):
        return remote(
            xrecv.at[0, i, d], line.at[i, d], as_s.at[i, d], ar_s.at[i, d],
            {"dp": lax.rem(s + data - nx, data)},
        )

    def emit(i, left, right):
        part[i] = dot(left, right, 0, 0).astype(BF).reshape(part.shape[1:])
        for k in range(1, nx):
            xcopy(i, k).start()

    @pl.loop(0, local)
    def _(e):
        rows_x = xs[:, slot_rows(e), :].reshape(blocks * CAP, width)
        rows_g = gs[:, slot_rows(e), :].reshape(blocks * CAP, width)
        emit(3 * e, rows_g, hid[e])
        gate, upv = gates[e], ups[e]
        sig = 1.0 / (1.0 + jnp.exp(-gate))
        gh = dot(rows_g, dw[e], 1, 0)
        gu = (gh * gate * sig).astype(BF)
        gg = (gh * upv * sig * (1.0 + gate * (1.0 - sig))).astype(BF)
        emit(3 * e + 1, rows_x, gg)
        emit(3 * e + 2, rows_x, gu)
        gin = dot(gg, gw[e], 1, 1) + dot(gu, uw[e], 1, 1)
        gins[:, slot_rows(e), :] = gin.astype(BF).reshape(blocks, CAP, width)
        outs[:, slot_rows(e), :] = dot(hid[e], dw[e], 1, 1).astype(BF).reshape(blocks, CAP, width)

    @pl.loop(0, blocks)
    def _(b):
        mixed[b] = dot(cmat[b], outs[b], 0, 0).astype(BF).reshape(mixed.shape[1:])
        gtok[b] = dot(dmat[b], gins[b], 0, 0).astype(BF)

    backs, grad_backs, talks = [], [], []
    for k in range(1, experts):
        peer = lax.rem(c + k, experts)
        backs.append(
            remote(mixed.at[peer], mrecv.at[k - 1], bks.at[k - 1], bkr.at[k - 1], {"expert": peer})
        )
        backs[-1].start()
    for k in range(1, experts):
        peer = lax.rem(c + k, experts)
        grad_backs.append(
            remote(gtok.at[peer], grecv.at[k - 1], gks.at[k - 1], gkr.at[k - 1], {"expert": peer})
        )
        grad_backs[-1].start()

    def step(i):
        @pl.when(i < chunks)
        def _():
            for k in range(1, nx):
                xcopy(i, k).wait_recv()
            for d in range(nz):
                held = part[i, d, x].astype(F32)
                for k in range(1, nx):
                    held = held + xrecv[k - 1, i, d].astype(F32)
                xrecv[0, i, d] = held.astype(BF)

        rise = i - z

        @pl.when((rise >= 0) & (rise < chunks))
        def _():
            for d in range(1, nz):
                @pl.when((z > 0) & (z < d))
                def _():
                    upcopy(rise, d).wait_recv()
                    xrecv[0, rise, d] = (
                        xrecv[0, rise, d].astype(F32) + line[rise, d + 1].astype(F32)
                    ).astype(BF)

                @pl.when(z < d)
                def _():
                    upcopy(rise, d).start()

        fall = i - (nz - 1 - z)

        @pl.when((fall >= 0) & (fall < chunks))
        def _():
            for d in range(nz - 1):
                @pl.when((z < nz - 1) & (z > d))
                def _():
                    downcopy(fall, d).wait_recv()
                    xrecv[0, fall, d] = (
                        xrecv[0, fall, d].astype(F32) + line[fall, d].astype(F32)
                    ).astype(BF)

                @pl.when(z > d)
                def _():
                    downcopy(fall, d).start()

        last = i - (nz - 1)

        @pl.when(last >= 0)
        def _():
            acc[...] = xrecv[0, last, z].astype(F32)

            @pl.when(z > 0)
            def _():
                upcopy(last, z).wait_recv()
                acc[...] += line[last, z + 1].astype(F32)

            @pl.when(z < nz - 1)
            def _():
                downcopy(last, z).wait_recv()
                acc[...] += line[last, z].astype(F32)

            e = lax.div(last, 3)
            for m, out in enumerate((out_down, out_gate, out_up)):
                @pl.when(lax.rem(last, 3) == m)
                def _():
                    out[e] = acc[...] * (1.0 / data)

    early = min(3, chunks)
    pl.loop(0, early)(step)

    for copy in backs:
        copy.wait_recv()
    held = mixed[c].astype(F32)
    for k in range(experts - 1):
        held = held + mrecv[k].astype(F32)
    msum[...] = held.astype(BF)
    for k in range(1, data):
        peer = lax.rem(s + k, data)
        talks.append(remote(msum.at[peer], talk.at[s], tks.at[k - 1], tkr.at[k - 1], {"dp": peer}))
        talks[-1].start()
    talk[s] = msum[s]
    for copy in grad_backs:
        copy.wait_recv()
    held = gtok[c].astype(F32)
    for k in range(experts - 1):
        held = held + grecv[k].astype(F32)
    grads[...] = held.astype(BF)

    pl.loop(early, chunks + nz - 1)(step)

    for copy in owner_grads + metas + tok_sent + tok_passed + up_sent + up_passed:
        copy.wait_send()
    for copy in backs + grad_backs:
        copy.wait_send()
    for copy in talks:
        copy.wait()

    @pl.loop(0, chunks)
    def _(i):
        for k in range(1, nx):
            xcopy(i, k).wait_send()
        for d in range(nz):
            @pl.when(d > z)
            def _():
                upcopy(i, d).wait_send()

            @pl.when(d < z)
            def _():
                downcopy(i, d).wait_send()


def layer(tokens, meta, owner_grads, gate_weight, up_weight, down_weight):
    experts, data = lax.axis_size("expert"), lax.axis_size("dp")
    nx = 1 << ((data.bit_length() - 1) // 2)
    nz = data // nx
    local, width, ff = gate_weight.shape
    rows, _ = tokens.shape
    per_owner = rows // data
    chunks, piece = 3 * local, width // data
    slots = local * CAP
    half = experts // 2
    grad_shape = jax.ShapeDtypeStruct((local, piece, ff), F32)
    dma = pltpu.SemaphoreType.DMA
    mem = pltpu.VMEM
    hbm = pl.BlockSpec(memory_space=pl.ANY)
    two = lambda *shape: [dma(shape), dma(shape)]
    return pl.pallas_call(
        functools.partial(layer_kernel, experts, nz, nx),
        out_shape=(
            grad_shape,
            grad_shape,
            grad_shape,
            jax.ShapeDtypeStruct((data, per_owner, width), BF),
            jax.ShapeDtypeStruct((rows, width), BF),
        ),
        in_specs=[VMEM] * 3 + [hbm] * 3,
        out_specs=(VMEM,) * 5,
        scratch_shapes=[
            mem((experts, rows, width), BF),
            mem((experts,) + meta.shape, F32),
            mem((experts, data, per_owner, width), BF),
            mem((local, width, ff), BF),
            mem((local, width, ff), BF),
            mem((local, width, ff), BF),
            mem((experts, slots, rows), BF),
            mem((experts, slots, rows), BF),
            mem((experts, slots, width), BF),
            mem((experts, slots, width), BF),
            mem((experts, slots, width), BF),
            mem((experts, slots, width), BF),
            mem((local, experts * CAP, ff), F32),
            mem((local, experts * CAP, ff), F32),
            mem((local, experts * CAP, ff), BF),
            mem((experts, data, per_owner, width), BF),
            mem((experts, rows, width), BF),
            mem((chunks, nz, nx, piece, ff), BF),
            mem((nx - 1, chunks, nz, piece, ff), BF),
            mem((chunks, nz + 1, piece, ff), BF),
            mem((experts - 1, data, per_owner, width), BF),
            mem((experts - 1, rows, width), BF),
            mem((data, per_owner, width), BF),
            mem((piece, ff), F32),
            dma((3,)),
        ]
        + two(data - 1)
        + two(half)
        + two(half)
        + two(experts - 1)
        + two(half)
        + two(half)
        + two(nx - 1, chunks)
        + two(chunks, nz)
        + two(chunks, nz)
        + two(experts - 1)
        + two(experts - 1)
        + two(data - 1),
        compiler_params=pltpu.CompilerParams(
            collective_id=0, has_side_effects=True, vmem_limit_bytes=62 * 2**20
        ),
    )(tokens, meta, owner_grads, gate_weight, up_weight, down_weight)


def on_device(
    tokens,
    expert_ids,
    slot_index,
    combine_weight,
    talker_owner,
    gate_weight,
    up_weight,
    down_weight,
    grad_talker,
):
    data = lax.axis_size("dp")
    rows, width = tokens.shape
    per_owner = rows // data
    order = jnp.arange(rows, dtype=jnp.int32)
    same = (talker_owner[:, None] == talker_owner[None, :]) & (order[:, None] < order[None, :])
    owner_slot = talker_owner * per_owner + jnp.sum(same.astype(jnp.int32), axis=0)
    position = jnp.where(slot_index >= 0, expert_ids * CAP + slot_index, -1).astype(F32).T
    weight = combine_weight.astype(F32).T
    pick = owner_slot[None, :] == order[:, None]
    moved = jnp.sum(
        jnp.where(pick[None], jnp.concatenate([position, weight], 0)[:, None, :], 0.0), axis=2
    )
    meta = jnp.concatenate([position, moved], 0)
    grad_gate, grad_up, grad_down, talk, grad_tokens = layer(
        tokens,
        meta,
        grad_talker.reshape(data, per_owner, width),
        gate_weight,
        up_weight,
        down_weight,
    )
    return (talk.reshape(rows, width), grad_tokens, grad_gate, grad_up, grad_down)


def solution(mesh):
    placed = (
        P(("dp", "expert"), None),
        P(("dp", "expert"), None),
        P(("dp", "expert"), None),
        P(("dp", "expert"), None),
        P(("dp", "expert")),
        P("expert", None, None),
        P("expert", None, None),
        P("expert", None, None),
        P(("dp", "expert"), None),
    )
    return jax.shard_map(
        on_device,
        mesh=mesh,
        in_specs=placed,
        out_specs=(
            P(("dp", "expert"), None),
            P(("dp", "expert"), None),
            P("expert", "dp", None),
            P("expert", "dp", None),
            P("expert", "dp", None),
        ),
        check_vma=False,
    )
```

time: 189 us -> 161 us (0.85)
  Pallas kernels: 179 us -> 149 us
  local copies, waits for them, and re-layouts: 4.53 us -> 7.29 us
    pallas_call x3 -> x1, Pallas kernels: 179 us -> 149 us  [layer(): pl.pallas_call(functools.partial(layer_kernel, experts, nz, nx), out_shap...]
    unnamed x6 -> x9, local copies, waits for them, and re-layouts: 1.41 us -> 7.29 us
    slice x1 -> x0, local copies, waits for them, and re-layouts: 3.11 us -> none  [on_device(): total[2 * local:]]
where the time goes in v2:
time: 161 us
  Pallas kernels  149 us (93%)
  local copies, waits for them, and re-layouts  7.29 us (5%)
  other arithmetic  3.85 us (2%)
    pallas_call x1, Pallas kernels, layer(): pl.pallas_call(functools.partial(layer_kernel, experts, nz, nx), out_shap...  149 us
    unnamed x9, local copies, waits for them, and re-layouts  7.29 us

profile of v2, /device:TPU:0, one launch (start us, length us, event | category | flops | bytes accessed | tf_op | source)
XLA Modules:
  0.0 160.8 jit_solution(15511949939358950693)
XLA Ops:
  0.6 0.8 convert_reduce_fusion
  1.5 0.7 multiply_add_fusion
  2.1 0.7 convert_bitcast_fusion.1
  2.8 0.7 convert_bitcast_fusion
  3.5 0.3 select_reduce_fusion
  3.9 0.6 pad_maximum_fusion.meta
  4.5 149.0 %shard_map.128 = (f32[4,128,384]{2,1,0:T(8,128)}, f32[4,128,384]{2,1,0:T(8,128)}, f32[4,128,384]{2,1,0:T(8,128)}, bf16[8,16,1024]{2,1,0:T(8,128)(2,1)}, bf16[128,1024]{1,0:T(8,128)(2,1)}) custom-call(bf16[128,1024]{1,0:T(8,128)(2,1)} %tok.1, f32[24,128]{1,0:T(8,128)} %pad_maximum_fusion.meta, bf16[8,16,1024]{2,1,0:T(8,128)(2,1)} %bitcast.7, ...), custom_call_target="tpu_custom_call" | custom-call | tf_op jit(solution)/shard_map/pallas_call | solution.py:349
  153.5 0.0 copy-start.1
  153.5 0.0 copy-start
  153.5 1.8 %copy.19 = bf16[128,1024]{1,0:T(8,128)(2,1)} copy(bf16[128,1024]{1,0:T(8,128)(2,1)} %bitcast.6) | data formatting | bytes 524288
  155.3 1.7 %copy.20 = bf16[128,1024]{1,0:T(8,128)(2,1)} copy(bf16[128,1024]{1,0:T(8,128)(2,1)} %get-tuple-element.21) | data formatting | bytes 524288
  156.9 2.1 %copy.21 = f32[4,128,384]{2,1,0:T(8,128)} copy(f32[4,128,384]{2,1,0:T(8,128)} %get-tuple-element.22) | data formatting | bytes 1572864
  159.0 0.0 copy-done.1
  159.0 0.9 copy.22
  159.9 0.0 copy-done
  159.9 0.9 copy.23
  (2 shorter events, 0.0 us)
Async XLA Ops:
  153.5 5.5 %copy-start.1 = (f32[4,128,384]{2,1,0:T(8,128)S(1)}, f32[4,128,384]{2,1,0:T(8,128)}, u32[]{:S(2)}) copy-start(f32[4,128,384]{2,1,0:T(8,128)} %get-tuple-element.23) | copy-start | bytes 2359300
  153.5 6.4 %copy-start = (f32[4,128,384]{2,1,0:T(8,128)S(1)}, f32[4,128,384]{2,1,0:T(8,128)}, u32[]{:S(2)}) copy-start(f32[4,128,384]{2,1,0:T(8,128)} %get-tuple-element.24) | copy-start | bytes 2359300

commit v3 on v2

--- a/solution.py
+++ b/solution.py
@@ -41,11 +41,11 @@
 
 def layer_kernel(
     experts, nz, nx, tok, meta, gt, gate_hbm, up_hbm, down_hbm,
-    out_gate, out_up, out_down, talk, grads,
+    total, talk, grads,
     tok_all, meta_all, up_all, gw, uw, dw, dmat, cmat, xs, gs, outs, gins, gates, ups, hid,
-    mixed, gtok, part, xrecv, line, mrecv, grecv, msum, acc,
+    mixed, gtok, part, xrecv, line, zline, xlast, mrecv, grecv, msum, acc,
     wsem, gs_s, gr_s, ts_s, tr_s, fs_s, fr_s, ms_s, mr_s, us_s, ur_s, vs_s, vr_s,
-    xs_s, xr_s, bs_s, br_s, as_s, ar_s, bks, bkr, gks, gkr, tks, tkr,
+    xs_s, xr_s, bs_s, br_s, as_s, ar_s, zb_s, zb_r, za_s, za_r, xl_s, xl_r, bks, bkr, gks, gkr, tks, tkr,
 ):
     data = nz * nx
     c, s = lax.axis_index("expert"), lax.axis_index("dp")
@@ -55,8 +55,9 @@
     local, width, ff = gw.shape
     blocks, rows, _ = tok_all.shape
     slots = local * CAP
-    pairs = meta.shape[0] // 3
+    pairs = meta.shape[0] // 4
     chunks = 3 * local
+    first = chunks // 6
 
     loads = [
         pltpu.make_async_copy(gate_hbm, gw, wsem.at[0]),
@@ -120,19 +121,30 @@
     base = (c * slots).astype(F32)
     want = lax.broadcasted_iota(jnp.int32, (slots, rows), 0).astype(F32) + base
 
+    wide = max(16, data)
+    kinds = lax.broadcasted_iota(jnp.int32, (wide, rows), 0).astype(F32)
+    line_of = lax.broadcasted_iota(jnp.int32, (rows, rows), 0)
+    earlier = (line_of < lax.broadcasted_iota(jnp.int32, (rows, rows), 1)).astype(F32).astype(BF)
+    line_of = line_of.astype(F32)
+
     @pl.loop(0, blocks)
     def _(b):
+        slot = meta_all[b, pairs : 2 * pairs, :]
+        place = jnp.where(slot >= 0.0, meta_all[b, 0:pairs, :] * CAP + slot, -1.0)
+        weight = meta_all[b, 2 * pairs : 3 * pairs, :]
         hit = jnp.zeros((slots, rows), F32)
         held = jnp.zeros((slots, rows), F32)
         for k in range(pairs):
-            hit = jnp.where(meta_all[b, k : k + 1, :] == want, 1.0, hit)
-            held = jnp.where(
-                meta_all[b, pairs + k : pairs + k + 1, :] == want,
-                meta_all[b, 2 * pairs + k : 2 * pairs + k + 1, :],
-                held,
-            )
+            here = place[k : k + 1, :] == want
+            hit = jnp.where(here, 1.0, hit)
+            held = jnp.where(here, weight[k : k + 1, :], held)
         dmat[b] = hit.astype(BF)
-        cmat[b] = held.astype(BF)
+        owner = meta_all[b, 3 * pairs : 3 * pairs + 1, :]
+        owned = (kinds == owner).astype(F32)
+        before = dot(owned.astype(BF), earlier, 1, 0)
+        owner_slot = owner * (rows // data) + jnp.sum(owned * before, axis=0, keepdims=True)
+        pick = (line_of == owner_slot).astype(F32).astype(BF)
+        cmat[b] = dot(held.astype(BF), pick, 1, 1).astype(BF)
 
     arrived(tok_sent, tok_passed)
 
@@ -182,10 +194,92 @@
             {"dp": lax.rem(s + data - nx, data)},
         )
 
+    def zup(i, d):
+        return remote(
+            part.at[i, d], zline.at[i, d + 1], zb_s.at[i, d], zb_r.at[i, d],
+            {"dp": lax.rem(s + nx, data)},
+        )
+
+    def zdown(i, d):
+        return remote(
+            part.at[i, d], zline.at[i, d], za_s.at[i, d], za_r.at[i, d],
+            {"dp": lax.rem(s + data - nx, data)},
+        )
+
+    def zlast(i, k):
+        px = lax.rem(x + k, nx)
+        return remote(
+            part.at[i, z, px], xlast.at[k - 1, i], xl_s.at[k - 1, i], xl_r.at[k - 1, i],
+            {"dp": z * nx + px},
+        )
+
     def emit(i, left, right):
         part[i] = dot(left, right, 0, 0).astype(BF).reshape(part.shape[1:])
-        for k in range(1, nx):
-            xcopy(i, k).start()
+
+        @pl.when(i >= first)
+        def _():
+            for k in range(1, nx):
+                xcopy(i, k).start()
+
+        if first:
+            for d in range(nz):
+                if d > 0:
+                    @pl.when((i < first) & (z == 0))
+                    def _():
+                        zup(i, d).start()
+
+                if d < nz - 1:
+                    @pl.when((i < first) & (z == nz - 1))
+                    def _():
+                        zdown(i, d).start()
+
+    def zstep(i):
+        rise = i - z
+
+        @pl.when((z > 0) & (rise >= 0) & (rise < first))
+        def _():
+            for d in range(1, nz):
+                @pl.when(z < d)
+                def _():
+                    zup(rise, d).wait_recv()
+                    part[rise, d] = (
+                        part[rise, d].astype(F32) + zline[rise, d + 1].astype(F32)
+                    ).astype(BF)
+                    zup(rise, d).start()
+
+        fall = i - (nz - 1 - z)
+
+        @pl.when((z < nz - 1) & (fall >= 0) & (fall < first))
+        def _():
+            for d in range(nz - 1):
+                @pl.when(z > d)
+                def _():
+                    zdown(fall, d).wait_recv()
+                    part[fall, d] = (
+                        part[fall, d].astype(F32) + zline[fall, d].astype(F32)
+                    ).astype(BF)
+                    zdown(fall, d).start()
+
+        last = i - (nz - 1)
+
+        @pl.when((last >= 0) & (last < first))
+        def _():
+            @pl.when(z > 0)
+            def _():
+                zup(last, z).wait_recv()
+                part[last, z] = (
+                    part[last, z].astype(F32) + zline[last, z + 1].astype(F32)
+                ).astype(BF)
+
+            @pl.when(z < nz - 1)
+            def _():
+                zdown(last, z).wait_recv()
+                part[last, z] = (
+                    part[last, z].astype(F32) + zline[last, z].astype(F32)
+                ).astype(BF)
+
+            for k in range(1, nx):
+                zlast(last, k).start()
 
     @pl.loop(0, local)
     def _(e):
@@ -223,7 +317,10 @@
         grad_backs[-1].start()
 
     def step(i):
-        @pl.when(i < chunks)
+        if first:
+            zstep(i)
+
+        @pl.when((i >= first) & (i < chunks))
         def _():
             for k in range(1, nx):
                 xcopy(i, k).wait_recv()
@@ -235,7 +332,7 @@
 
         rise = i - z
 
-        @pl.when((rise >= 0) & (rise < chunks))
+        @pl.when((rise >= first) & (rise < chunks))
         def _():
             for d in range(1, nz):
                 @pl.when((z > 0) & (z < d))
@@ -251,7 +348,7 @@
 
         fall = i - (nz - 1 - z)
 
-        @pl.when((fall >= 0) & (fall < chunks))
+        @pl.when((fall >= first) & (fall < chunks))
         def _():
             for d in range(nz - 1):
                 @pl.when((z < nz - 1) & (z > d))
@@ -267,7 +364,7 @@
 
         last = i - (nz - 1)
 
-        @pl.when(last >= 0)
+        @pl.when(last >= first)
         def _():
             acc[...] = xrecv[0, last, z].astype(F32)
 
@@ -281,13 +378,10 @@
                 downcopy(last, z).wait_recv()
                 acc[...] += line[last, z].astype(F32)
 
-            e = lax.div(last, 3)
-            for m, out in enumerate((out_down, out_gate, out_up)):
-                @pl.when(lax.rem(last, 3) == m)
-                def _():
-                    out[e] = acc[...] * (1.0 / data)
-
-    early = min(3, chunks)
+            total[lax.rem(last, 3) * local + lax.div(last, 3)] = acc[...] * (1.0 / data)
+
+    early = min(first + 3, chunks)
+    late = chunks - 1
     pl.loop(0, early)(step)
 
     for copy in backs:
@@ -308,7 +402,16 @@
         held = held + grecv[k].astype(F32)
     grads[...] = held.astype(BF)
 
-    pl.loop(early, chunks + nz - 1)(step)
+    pl.loop(early, late)(step)
+
+    for i in range(first):
+        held = part[i, z, x].astype(F32)
+        for k in range(1, nx):
+            zlast(i, k).wait_recv()
+            held = held + xlast[k - 1, i].astype(F32)
+        total[i % 3 * local + i // 3] = held * (1.0 / data)
+
+    pl.loop(max(early, late), chunks + nz - 1)(step)
 
     for copy in owner_grads + metas + tok_sent + tok_passed + up_sent + up_passed:
         copy.wait_send()
@@ -317,7 +420,7 @@
     for copy in talks:
         copy.wait()
 
-    @pl.loop(0, chunks)
+    @pl.loop(first, chunks)
     def _(i):
         for k in range(1, nx):
             xcopy(i, k).wait_send()
@@ -329,6 +432,18 @@
             @pl.when(d < z)
             def _():
                 downcopy(i, d).wait_send()
+
+    for i in range(first):
+        for k in range(1, nx):
+            zlast(i, k).wait_send()
+        for d in range(nz):
+            @pl.when(d > z)
+            def _():
+                zup(i, d).wait_send()
+
+            @pl.when(d < z)
+            def _():
+                zdown(i, d).wait_send()
 
 
 def layer(tokens, meta, owner_grads, gate_weight, up_weight, down_weight):
@@ -339,9 +454,9 @@
     rows, _ = tokens.shape
     per_owner = rows // data
     chunks, piece = 3 * local, width // data
+    lead = max(1, chunks // 6)
     slots = local * CAP
     half = experts // 2
-    grad_shape = jax.ShapeDtypeStruct((local, piece, ff), F32)
     dma = pltpu.SemaphoreType.DMA
     mem = pltpu.VMEM
     hbm = pl.BlockSpec(memory_space=pl.ANY)
@@ -349,14 +464,12 @@
     return pl.pallas_call(
         functools.partial(layer_kernel, experts, nz, nx),
         out_shape=(
-            grad_shape,
-            grad_shape,
-            grad_shape,
+            jax.ShapeDtypeStruct((chunks, piece, ff), F32),
             jax.ShapeDtypeStruct((data, per_owner, width), BF),
             jax.ShapeDtypeStruct((rows, width), BF),
         ),
         in_specs=[VMEM] * 3 + [hbm] * 3,
-        out_specs=(VMEM,) * 5,
+        out_specs=(VMEM,) * 3,
         scratch_shapes=[
             mem((experts, rows, width), BF),
             mem((experts,) + meta.shape, F32),
@@ -378,6 +491,8 @@
             mem((chunks, nz, nx, piece, ff), BF),
             mem((nx - 1, chunks, nz, piece, ff), BF),
             mem((chunks, nz + 1, piece, ff), BF),
+            mem((lead, nz + 1, nx, piece, ff), BF),
+            mem((nx - 1, lead, piece, ff), BF),
             mem((experts - 1, data, per_owner, width), BF),
             mem((experts - 1, rows, width), BF),
             mem((data, per_owner, width), BF),
@@ -393,6 +508,9 @@
         + two(nx - 1, chunks)
         + two(chunks, nz)
         + two(chunks, nz)
+        + two(lead, nz)
+        + two(lead, nz)
+        + two(nx - 1, lead)
         + two(experts - 1)
         + two(experts - 1)
         + two(data - 1),
@@ -416,17 +534,17 @@
     data = lax.axis_size("dp")
     rows, width = tokens.shape
     per_owner = rows // data
-    order = jnp.arange(rows, dtype=jnp.int32)
-    same = (talker_owner[:, None] == talker_owner[None, :]) & (order[:, None] < order[None, :])
-    owner_slot = talker_owner * per_owner + jnp.sum(same.astype(jnp.int32), axis=0)
-    position = jnp.where(slot_index >= 0, expert_ids * CAP + slot_index, -1).astype(F32).T
-    weight = combine_weight.astype(F32).T
-    pick = owner_slot[None, :] == order[:, None]
-    moved = jnp.sum(
-        jnp.where(pick[None], jnp.concatenate([position, weight], 0)[:, None, :], 0.0), axis=2
-    )
-    meta = jnp.concatenate([position, moved], 0)
-    grad_gate, grad_up, grad_down, talk, grad_tokens = layer(
+    pairs = expert_ids.shape[1]
+    meta = jnp.concatenate(
+        [
+            expert_ids.astype(F32),
+            slot_index.astype(F32),
+            combine_weight.astype(F32),
+            jnp.broadcast_to(talker_owner.astype(F32)[:, None], (rows, pairs)),
+        ],
+        1,
+    ).T
+    total, talk, grad_tokens = layer(
         tokens,
         meta,
         grad_talker.reshape(data, per_owner, width),
@@ -434,7 +552,14 @@
         up_weight,
         down_weight,
     )
-    return (talk.reshape(rows, width), grad_tokens, grad_gate, grad_up, grad_down)
+    local = gate_weight.shape[0]
+    return (
+        talk.reshape(rows, width),
+        grad_tokens,
+        total[local : 2 * local],
+        total[2 * local :],
+        total[:local],
+    )
 
 
 def solution(mesh):

time: 161 us -> 147 us (0.913)
  Pallas kernels: 149 us -> 138 us
  local copies, waits for them, and re-layouts: 7.29 us -> 4.53 us
    pallas_call x1, Pallas kernels: 149 us -> 138 us  [layer(): pl.pallas_call(functools.partial(layer_kernel, experts, nz, nx), out_shap...]
    unnamed x9 -> x6, local copies, waits for them, and re-layouts: 7.29 us -> 1.41 us
    slice x0 -> x1, local copies, waits for them, and re-layouts: none -> 3.11 us  [on_device(): total[:local]]
    convert_element_type x0 -> x4, other arithmetic: none -> 2.72 us  [the longest x1 0.69 us: on_device(): expert_ids.astype(F32)]
where the time goes in v3:
time: 147 us
  Pallas kernels  138 us (94%)
  local copies, waits for them, and re-layouts  4.53 us (3%)
  other arithmetic  3.33 us (2%)
    pallas_call x1, Pallas kernels, layer(): pl.pallas_call(functools.partial(layer_kernel, experts, nz, nx), out_shap...  138 us
    slice x1, local copies, waits for them, and re-layouts, on_device(): total[:local]  3.11 us

profile of v3, /device:TPU:0, one launch (start us, length us, event | category | flops | bytes accessed | tf_op | source)
XLA Modules:
  0.0 146.6 jit_solution(523532786217511661)
XLA Ops:
  0.6 0.7 convert_element_type.15
  1.3 0.7 convert_element_type.12
  2.0 0.7 convert_element_type.13
  2.7 0.7 convert_element_type.14
  3.4 0.6 maximum_bitcast_fusion.meta
  4.0 138.1 %shard_map.128 = (f32[12,128,384]{2,1,0:T(8,128)}, bf16[8,16,1024]{2,1,0:T(8,128)(2,1)}, bf16[128,1024]{1,0:T(8,128)(2,1)}) custom-call(bf16[128,1024]{1,0:T(8,128)(2,1)} %tok.1, f32[32,128]{1,0:T(8,128)} %maximum_bitcast_fusion.meta, bf16[8,16,1024]{2,1,0:T(8,128)(2,1)} %bitcast.4, bf16[4,1024,384]{2,1,0:T(8,128)(2,1)} %gate_hbm.1, ...), custom_call_target="tpu_custom_call" | custom-call | tf_op jit(solution)/shard_map/pallas_call | solution.py:464
  142.1 0.0 copy-start.1
  142.1 0.0 copy-start
  142.1 3.1 %fusion = (f32[4,128,384]{2,1,0:T(8,128)}, f32[4,128,384]{2,1,0:T(8,128)}, f32[4,128,384]{2,1,0:T(8,128)}) fusion(f32[12,128,384]{2,1,0:T(8,128)} %get-tuple-element.10), kind=kLoop, calls=%fused_computation.1 | loop fusion | bytes 4718592 | tf_op jit(solution)/shard_map/slice | solution.py:561
  145.2 0.0 copy-done.1
  145.2 0.7 copy.16
  145.9 0.0 copy-done
  145.9 0.7 copy.17
  (1 shorter events, 0.0 us)
Async XLA Ops:
  142.1 3.1 %copy-start.1 = (bf16[8,16,1024]{2,1,0:T(8,128)(2,1)S(1)}, bf16[8,16,1024]{2,1,0:T(8,128)(2,1)}, u32[]{:S(2)}) copy-start(bf16[8,16,1024]{2,1,0:T(8,128)(2,1)} %get-tuple-element.8) | copy-start | bytes 786436
  142.1 3.8 %copy-start = (bf16[128,1024]{1,0:T(8,128)(2,1)S(1)}, bf16[128,1024]{1,0:T(8,128)(2,1)}, u32[]{:S(2)}) copy-start(bf16[128,1024]{1,0:T(8,128)(2,1)} %get-tuple-element.20) | copy-start | bytes 786436

commit v4 on v3

--- a/solution.py
+++ b/solution.py
@@ -40,9 +40,9 @@
 
 
 def layer_kernel(
-    experts, nz, nx, tok, meta, gt, gate_hbm, up_hbm, down_hbm,
+    experts, nz, nx, tok, ids, slot_ids, shares, owners, gt, gate_hbm, up_hbm, down_hbm,
     total, talk, grads,
-    tok_all, meta_all, up_all, gw, uw, dw, dmat, cmat, xs, gs, outs, gins, gates, ups, hid,
+    meta, tok_all, meta_all, up_all, gw, uw, dw, dmat, cmat, xs, gs, outs, gins, gates, ups, hid,
     mixed, gtok, part, xrecv, line, zline, xlast, mrecv, grecv, msum, acc,
     wsem, gs_s, gr_s, ts_s, tr_s, fs_s, fr_s, ms_s, mr_s, us_s, ur_s, vs_s, vr_s,
     xs_s, xr_s, bs_s, br_s, as_s, ar_s, zb_s, zb_r, za_s, za_r, xl_s, xl_r, bks, bkr, gks, gkr, tks, tkr,
@@ -103,11 +103,16 @@
             remote(gt.at[peer], up_all.at[c, s], gs_s.at[k - 1], gr_s.at[k - 1], {"dp": peer})
         )
         owner_grads[-1].start()
+    tok_sent = shared(tok, tok_all, ts_s, tr_s)
+    line_of = lax.broadcasted_iota(jnp.int32, (rows, rows), 0)
+    across = lax.broadcasted_iota(jnp.int32, (rows, rows), 1)
+    for k, table in enumerate((ids, slot_ids, shares)):
+        meta[k * pairs : (k + 1) * pairs, :] = table[...].astype(F32)
+    meta[3 * pairs :, :] = jnp.broadcast_to(owners[...].astype(F32), (pairs, rows))
     for k in range(1, experts):
         peer = {"expert": lax.rem(c + k, experts)}
         metas.append(remote(meta, meta_all.at[c], ms_s.at[k - 1], mr_s.at[k - 1], peer))
         metas[-1].start()
-    tok_sent = shared(tok, tok_all, ts_s, tr_s)
     tok_all[c] = tok[...]
     meta_all[c] = meta[...]
     up_all[c, s] = gt[s]
@@ -123,8 +128,7 @@
 
     wide = max(16, data)
     kinds = lax.broadcasted_iota(jnp.int32, (wide, rows), 0).astype(F32)
-    line_of = lax.broadcasted_iota(jnp.int32, (rows, rows), 0)
-    earlier = (line_of < lax.broadcasted_iota(jnp.int32, (rows, rows), 1)).astype(F32).astype(BF)
+    earlier = (line_of < across).astype(F32).astype(BF)
     line_of = line_of.astype(F32)
 
     @pl.loop(0, blocks)
@@ -152,7 +156,6 @@
     def _(b):
         xs[b] = dot(dmat[b], tok_all[b], 1, 0).astype(BF)
 
-    up_passed = passed(up_sent, up_all, vs_s, vr_s)
     for copy in loads:
         copy.wait()
 
@@ -169,6 +172,7 @@
         ups[e] = upv
         hid[e] = hidden
 
+    up_passed = passed(up_sent, up_all, vs_s, vr_s)
     arrived(up_sent, up_passed)
 
     @pl.loop(0, blocks)
@@ -446,13 +450,16 @@
                 zdown(i, d).wait_send()
 
 
-def layer(tokens, meta, owner_grads, gate_weight, up_weight, down_weight):
+def layer(
+    tokens, ids, slot_ids, shares, owners, owner_grads, gate_weight, up_weight, down_weight
+):
     experts, data = lax.axis_size("expert"), lax.axis_size("dp")
     nx = 1 << ((data.bit_length() - 1) // 2)
     nz = data // nx
     local, width, ff = gate_weight.shape
     rows, _ = tokens.shape
     per_owner = rows // data
+    pairs = ids.shape[0]
     chunks, piece = 3 * local, width // data
     lead = max(1, chunks // 6)
     slots = local * CAP
@@ -468,11 +475,12 @@
             jax.ShapeDtypeStruct((data, per_owner, width), BF),
             jax.ShapeDtypeStruct((rows, width), BF),
         ),
-        in_specs=[VMEM] * 3 + [hbm] * 3,
+        in_specs=[VMEM] * 6 + [hbm] * 3,
         out_specs=(VMEM,) * 3,
         scratch_shapes=[
+            mem((4 * pairs, rows), F32),
             mem((experts, rows, width), BF),
-            mem((experts,) + meta.shape, F32),
+            mem((experts, 4 * pairs, rows), F32),
             mem((experts, data, per_owner, width), BF),
             mem((local, width, ff), BF),
             mem((local, width, ff), BF),
@@ -517,7 +525,7 @@
         compiler_params=pltpu.CompilerParams(
             collective_id=0, has_side_effects=True, vmem_limit_bytes=62 * 2**20
         ),
-    )(tokens, meta, owner_grads, gate_weight, up_weight, down_weight)
+    )(tokens, ids, slot_ids, shares, owners, owner_grads, gate_weight, up_weight, down_weight)
 
 
 def on_device(
@@ -534,19 +542,12 @@
     data = lax.axis_size("dp")
     rows, width = tokens.shape
     per_owner = rows // data
-    pairs = expert_ids.shape[1]
-    meta = jnp.concatenate(
-        [
-            expert_ids.astype(F32),
-            slot_index.astype(F32),
-            combine_weight.astype(F32),
-            jnp.broadcast_to(talker_owner.astype(F32)[:, None], (rows, pairs)),
-        ],
-        1,
-    ).T
     total, talk, grad_tokens = layer(
         tokens,
-        meta,
+        expert_ids.T,
+        slot_index.T,
+        combine_weight.T,
+        talker_owner.reshape(1, rows),
         grad_talker.reshape(data, per_owner, width),
         gate_weight,
         up_weight,

time: 147 us -> 143 us (0.973)
  other arithmetic: 3.33 us -> 0 us
    convert_element_type x4 -> x0, other arithmetic: 2.72 us -> none  [the longest x1 0.69 us: on_device(): expert_ids.astype(F32)]
where the time goes in v4:
time: 143 us
  Pallas kernels  138 us (97%)
  local copies, waits for them, and re-layouts  4.53 us (3%)
    pallas_call x1, Pallas kernels, layer(): pl.pallas_call(functools.partial(layer_kernel, experts, nz, nx), out_shap...  138 us
    slice x1, local copies, waits for them, and re-layouts, on_device(): total[:local]  3.11 us

profile of v4, /device:TPU:0, one launch (start us, length us, event | category | flops | bytes accessed | tf_op | source)
XLA Modules:
  0.0 143.2 jit_solution(11332320067933319173)
XLA Ops:
  0.6 138.1 %shard_map.128 = (f32[12,128,384]{2,1,0:T(8,128)}, bf16[8,16,1024]{2,1,0:T(8,128)(2,1)}, bf16[128,1024]{1,0:T(8,128)(2,1)}) custom-call(bf16[128,1024]{1,0:T(8,128)(2,1)} %tok.1, s32[8,128]{1,0:T(8,128)} %bitcast.8, s32[8,128]{1,0:T(8,128)} %bitcast.9, bf16[8,128]{1,0:T(8,128)(2,1)} %bitcast.10, s32[1,128]{1,0:T(1,128)} %bitcast.11, ...), custom_call_target="tpu_custom_call" | custom-call | tf_op jit(solution)/shard_map/pallas_call | solution.py:471
  138.7 0.0 copy-start.1
  138.7 0.0 copy-start
  138.7 3.1 %fusion = (f32[4,128,384]{2,1,0:T(8,128)}, f32[4,128,384]{2,1,0:T(8,128)}, f32[4,128,384]{2,1,0:T(8,128)}) fusion(f32[12,128,384]{2,1,0:T(8,128)} %get-tuple-element.10), kind=kLoop, calls=%fused_computation | loop fusion | bytes 4718592 | tf_op jit(solution)/shard_map/slice | solution.py:562
  141.8 0.0 copy-done.1
  141.8 0.7 copy.16
  142.5 0.0 copy-done
  142.5 0.7 copy.17
Async XLA Ops:
  138.7 3.1 %copy-start.1 = (bf16[8,16,1024]{2,1,0:T(8,128)(2,1)S(1)}, bf16[8,16,1024]{2,1,0:T(8,128)(2,1)}, u32[]{:S(2)}) copy-start(bf16[8,16,1024]{2,1,0:T(8,128)(2,1)} %get-tuple-element.8) | copy-start | bytes 786436
  138.7 3.8 %copy-start = (bf16[128,1024]{1,0:T(8,128)(2,1)S(1)}, bf16[128,1024]{1,0:T(8,128)(2,1)}, u32[]{:S(2)}) copy-start(bf16[128,1024]{1,0:T(8,128)(2,1)} %get-tuple-element.20) | copy-start | bytes 786436
